TPU v7x, 128 devices: a whole 4x4x4 slice. The times are simulated.
128 devices in a mesh: ep: 16 (over z, x), fsdp: 8 (over y, core).
Axes of the slice: x: 4, y: 4, z: 4, core: 2. Of those that a mesh axis runs over, the one named last changes fastest.
Arguments:
- tokens: bfloat16 [4, 768, 2048], P(None, 'ep', 'fsdp'), may hold values from -6 to 6
- gate_up_weight: bfloat16 [128, 2048, 1536], P('ep', 'fsdp'), may hold values from -0.125 to 0.125
- down_weight: bfloat16 [128, 2048, 768], P('ep', 'fsdp'), may hold values from -0.21875 to 0.21875
- placement: int32 [160], replicated, may hold values from 0 to 127, as said below
- copy_ids: int32 [4, 768, 8], P(None, 'ep'), may hold values from 0 to 159, all different within a row; in each aligned block of 48 rows (0 to 47, 48 to 95, ..., all dimensions but the last counted through in order) at most 6 rows name the same one
- gate_codes: int32 [4, 768, 8], P(None, 'ep'), may hold values from 4 to 15
Outputs:
- mixed: bfloat16 [4, 768, 2048], P(None, 'ep', 'fsdp')
Inputs may be any that keep to these rules, and one draw needn't show every extreme that they name: `placement`: every expert has a copy, and the 10 copies held by one index of ep have experts e with different e // 8. `copy_ids`: the copies in a row differ; within the 48 rows of one index of ep in one step no copy is named by more than 6 rows.
All inputs are finite; a program needn't handle non-finite values.
Results may differ from a plain program's by a relative error of at most 0.023.
Values may be sent and summed in bfloat16 or wider, within the bound.
A program may use at most 128 MiB of HBM per device.

v0:
```python
import jax
import jax.numpy as jnp
from jax import lax
from jax.sharding import PartitionSpec as P

MOST = 6


def decode(
    tokens, copy_ids, gate_codes, dest_of, slot_of, groups, ep_count, weights_in, weights_out
):
    steps_count, rows_count, top_count = copy_ids.shape
    assigned = rows_count * top_count
    total_copies = dest_of.shape[0]
    flat_ids = copy_ids.reshape(steps_count, assigned)
    onehot = (
        flat_ids[:, :, None] == jnp.arange(total_copies, dtype=jnp.int32)[None, None, :]
    ).astype(jnp.int32)
    ranking = jnp.sum(jnp.cumsum(onehot, axis=1) * onehot, axis=2) - 1
    targets = jnp.sum(onehot * dest_of[None, None, :], axis=2)
    places = jnp.sum(onehot * slot_of[None, None, :], axis=2)
    step_index = jnp.arange(steps_count, dtype=jnp.int32)[:, None]
    slots = (((targets * groups + places) * steps_count + step_index) * MOST + ranking).reshape(-1)
    buffer_rows = ep_count * groups * steps_count * MOST
    everyone = steps_count * assigned
    inverse = (
        jnp.full((buffer_rows,), everyone, jnp.int32)
        .at[slots]
        .set(jnp.arange(everyone, dtype=jnp.int32))
    )
    valid = inverse < everyone
    source = jnp.minimum(inverse, everyone - 1) // top_count
    features = tokens.reshape(steps_count * rows_count, tokens.shape[2])
    outgoing = jnp.where(valid[:, None], features[source], jnp.zeros((), features.dtype))
    outgoing = outgoing.reshape(ep_count, groups, steps_count * MOST, features.shape[1])
    arrived = lax.all_to_all(outgoing, "ep", split_axis=0, concat_axis=2, tiled=True)[0]
    partial_value = jnp.einsum(
        "grd,gdh->grh", arrived, weights_in, preferred_element_type=jnp.float32
    ).astype(jnp.bfloat16)
    summed = lax.psum(partial_value, "fsdp").astype(jnp.float32)
    hidden_units = weights_out.shape[2]
    hidden = (jax.nn.silu(summed[..., :hidden_units]) * summed[..., hidden_units:]).astype(
        jnp.bfloat16
    )
    result = jnp.einsum(
        "grh,gdh->grd", hidden, weights_out, preferred_element_type=jnp.float32
    ).astype(jnp.bfloat16)
    returned = lax.all_to_all(result[None], "ep", split_axis=2, concat_axis=0, tiled=True)
    values = returned.reshape(buffer_rows, features.shape[1])[slots]
    values = values.reshape(steps_count, rows_count, top_count, features.shape[1])
    weights = gate_codes.astype(jnp.float32)
    weights = weights / jnp.sum(weights, axis=2, keepdims=True)
    return jnp.sum(values.astype(jnp.float32) * weights[..., None], axis=2).astype(jnp.bfloat16)


def local(tokens, gate_up_weight, down_weight, placement, copy_ids, gate_codes):
    ep_count = lax.axis_size("ep")
    own_index = lax.axis_index("ep")
    experts_local = gate_up_weight.shape[0]
    total_copies = placement.shape[0]
    per_holder = total_copies // ep_count
    owners = placement // experts_local
    local_ids = placement % experts_local
    holders = jnp.arange(total_copies, dtype=jnp.int32) // per_holder
    matches = (holders[None, :] == jnp.arange(ep_count, dtype=jnp.int32)[:, None]) & (
        owners[None, :] == own_index
    )
    present = jnp.any(matches, axis=1)
    picked = jnp.sum(jnp.where(matches, local_ids[None, :], 0), axis=1)
    chosen_in = jnp.where(
        present[:, None, None], gate_up_weight[picked], jnp.zeros((), gate_up_weight.dtype)
    )
    chosen_out = jnp.where(
        present[:, None, None], down_weight[picked], jnp.zeros((), down_weight.dtype)
    )
    moved_in, moved_out = (
        lax.all_to_all(chosen_in, "ep", split_axis=0, concat_axis=0, tiled=True),
        lax.all_to_all(chosen_out, "ep", split_axis=0, concat_axis=0, tiled=True),
    )
    mine = lax.dynamic_slice_in_dim(owners, own_index * per_holder, per_holder)
    weights_in = moved_in[mine]
    weights_out = moved_out[mine]
    slot_of = jnp.arange(total_copies, dtype=jnp.int32) % per_holder
    outputs = []
    for step_index in range(tokens.shape[0]):
        outputs.append(
            decode(
                tokens[step_index : step_index + 1],
                copy_ids[step_index : step_index + 1],
                gate_codes[step_index : step_index + 1],
                holders,
                slot_of,
                per_holder,
                ep_count,
                weights_in,
                weights_out,
            )
        )
    mixed = jnp.concatenate(outputs, axis=0)
    return mixed


def solution(mesh):
    in_specs = (
        P(None, "ep", "fsdp"),
        P("ep", "fsdp", None),
        P("ep", "fsdp", None),
        P(),
        P(None, "ep", None),
        P(None, "ep", None),
    )
    out_specs = P(None, "ep", "fsdp")
    return jax.shard_map(local, mesh=mesh, in_specs=in_specs, out_specs=out_specs, check_vma=False)
```

profile of v0, /device:TPU:8, one launch (start us, length us, event | category | flops | bytes accessed | tf_op | source)
XLA Modules:
  0.0 635.8 jit_solution(10307598395228741361)
XLA Ops:
  73.1 4.9 gather_fusion
  82.4 7.9 %all-to-all-start = ((bf16[16,10,6,256]{3,2,1,0:T(8,128)(2,1)}), bf16[16,10,6,256]{3,2,1,0:T(8,128)(2,1)}, u32[]{:S(2)}, u32[]{:S(2)}) async-start(bf16[16,10,6,256]{3,2,1,0:T(8,128)(2,1)} %broadcast_select_fusion.5), calls=%async_computation | async-start | bytes 1310720 | tf_op jit(solution)/shard_map/all_to_all | solution.py:36
  99.6 4.9 gather_fusion.6
  106.7 4.9 gather_fusion.8
  123.3 7.2 %all-to-all-start.4 = ((bf16[16,10,6,256]{3,2,1,0:T(8,128)(2,1)}), bf16[16,10,6,256]{3,2,1,0:T(8,128)(2,1)}, u32[]{:S(2)}, u32[]{:S(2)}) async-start(bf16[16,10,6,256]{3,2,1,0:T(8,128)(2,1)} %broadcast_select_fusion.4), calls=%async_computation.4 | async-start | bytes 1310720 | tf_op jit(solution)/shard_map/all_to_all | solution.py:36
  132.7 10.2 %all-to-all-done.4 = bf16[16,10,6,256]{3,2,1,0:T(8,128)(2,1)} async-done(((bf16[16,10,6,256]{3,2,1,0:T(8,128)(2,1)}), bf16[16,10,6,256]{3,2,1,0:T(8,128)(2,1)}, u32[]{:S(2)}, u32[]{:S(2)}) %all-to-all-start.4) | async-done | bytes 491552 | tf_op jit(solution)/shard_map/all_to_all | solution.py:36
  147.3 9.2 %gather_fusion.1 = bf16[16,256,1536]{2,1,0:T(8,128)(2,1)} fusion(bf16[8,256,1536]{2,1,0:T(8,128)(2,1)} %param.7, s32[1024]{0:T(1024)S(1)} %pad_clamp_fusion.8), kind=kCustom, calls=%fused_computation.1 | custom fusion | bytes 25165888 | tf_op jit(solution)/shard_map/gather | solution.py:71
  158.9 7.1 %all-to-all-start.8 = ((bf16[16,10,6,256]{3,2,1,0:T(8,128)(2,1)}), bf16[16,10,6,256]{3,2,1,0:T(8,128)(2,1)}, u32[]{:S(2)}, u32[]{:S(2)}) async-start(bf16[16,10,6,256]{3,2,1,0:T(8,128)(2,1)} %broadcast_select_fusion.2), calls=%async_computation.8 | async-start | bytes 1310720 | tf_op jit(solution)/shard_map/all_to_all | solution.py:36
  165.9 10.7 %broadcast_select_fusion = bf16[16,256,1536]{2,1,0:T(8,128)(2,1)} fusion(bf16[16,256,1536]{2,1,0:T(8,128)(2,1)} %gather_fusion.1, pred[16]{0:T(512)(128)(4,1)S(1)} %fusion.45), kind=kLoop, calls=%fused_computation.16 | loop fusion | flops 6291456 | bytes 25165840 | tf_op jit(solution)/shard_map/jit(_where)/select_n | solution.py:70
  177.0 6.8 %all-to-all-start.1 = ((bf16[16,256,1536]{2,1,0:T(8,128)(2,1)}), bf16[16,256,1536]{2,1,0:T(8,128)(2,1)}, u32[]{:S(2)}, u32[]{:S(2)}) async-start(bf16[16,256,1536]{2,1,0:T(8,128)(2,1)} %broadcast_select_fusion), calls=%async_computation.1 | async-start | bytes 25165824 | tf_op jit(solution)/shard_map/all_to_all | solution.py:77
  187.6 5.9 broadcast_select_fusion.1
  198.7 165.7 %all-to-all-done.1 = bf16[16,256,1536]{2,1,0:T(8,128)(2,1)} async-done(((bf16[16,256,1536]{2,1,0:T(8,128)(2,1)}), bf16[16,256,1536]{2,1,0:T(8,128)(2,1)}, u32[]{:S(2)}, u32[]{:S(2)}) %all-to-all-start.1) | async-done | bytes 12582944 | tf_op jit(solution)/shard_map/all_to_all | solution.py:77
  364.4 4.9 all-to-all-start.2
  369.6 9.6 %gather_fusion.2 = bf16[10,256,1536]{2,1,0:T(8,128)(2,1)} fusion(bf16[16,256,1536]{2,1,0:T(8,128)(2,1)} %all-to-all-done.1, s32[1024]{0:T(1024)S(1)} %pad_clamp_fusion.7), kind=kCustom, calls=%fused_computation.2 | custom fusion | bytes 15728680 | tf_op jit(solution)/shard_map/gather | solution.py:81
  379.2 6.4 %convolution_convert_fusion.3 = bf16[10,96,1536]{2,1,0:T(8,128)(2,1)} fusion(bf16[10,96,256]{2,1,0:T(8,128)(2,1)S(1)} %squeeze.12, bf16[10,256,1536]{2,1,0:T(8,128)(2,1)} %gather_fusion.2), kind=kOutput, calls=%fused_computation.21 | convolution fusion | flops 756449280 | bytes 11304960 | tf_op jit(solution)/shard_map/grd,gdh->grh/dot_general | solution.py:37
  395.3 58.4 %all-to-all-done.2 = bf16[16,256,768]{2,1,0:T(8,128)(2,1)} async-done(((bf16[16,256,768]{2,1,0:T(8,128)(2,1)}), bf16[16,256,768]{2,1,0:T(8,128)(2,1)}, u32[]{:S(2)}, u32[]{:S(2)}) %all-to-all-start.2) | async-done | bytes 6291488 | tf_op jit(solution)/shard_map/all_to_all | solution.py:78
  453.7 5.8 gather_fusion.4
  459.4 70.8 %all-reduce.3.cloned.1.call-done = (bf16[10,96,1536]{2,1,0:T(8,128)(2,1)}, bf16[10,96,1536]{2,1,0:T(8,128)(2,1)}, bf16[10,96,1536]{2,1,0:T(8,128)(2,1)}, bf16[10,96,1536]{2,1,0:T(8,128)(2,1)}) async-done(((bf16[10,96,1536]{2,1,0:T(8,128)(2,1)}, bf16[10,96,1536]{2,1,0:T(8,128)(2,1)}, bf16[10,96,1536]{2,1,0:T(8,128)(2,1)}, bf16[10,96,1536]{2,1,0:T(8,128)(2,1)}), (bf16[10,96,1536]{2,1,0:T(8,128)(2,1)}, ...) | async-done | bytes 11796496 | tf_op jit(solution)/shard_map/psum | solution.py:40
  535.9 7.2 %all-to-all-start.3 = ((bf16[1,10,96,256]{3,1,0,2:T(8,128)(2,1)}), bf16[1,10,96,256]{3,1,0,2:T(8,128)(2,1)S(1)}, u32[]{:S(2)}, u32[]{:S(2)}) async-start(bf16[1,10,96,256]{3,1,0,2:T(8,128)(2,1)} %copy.116), calls=%async_computation.3 | async-start | bytes 1572864 | tf_op jit(solution)/shard_map/all_to_all | solution.py:48
  552.0 7.6 %all-to-all-done.3 = bf16[1,10,96,256]{3,1,0,2:T(8,128)(2,1)S(1)} async-done(((bf16[1,10,96,256]{3,1,0,2:T(8,128)(2,1)}), bf16[1,10,96,256]{3,1,0,2:T(8,128)(2,1)S(1)}, u32[]{:S(2)}, u32[]{:S(2)}) %all-to-all-start.3) | async-done | bytes 491552 | tf_op jit(solution)/shard_map/all_to_all | solution.py:48
  563.4 5.4 fusion.30
  581.9 5.2 fusion.33
  588.3 7.4 %all-to-all-done.7 = bf16[1,10,96,256]{3,1,0,2:T(8,128)(2,1)S(1)} async-done(((bf16[1,10,96,256]{3,1,0,2:T(8,128)(2,1)}), bf16[1,10,96,256]{3,1,0,2:T(8,128)(2,1)S(1)}, u32[]{:S(2)}, u32[]{:S(2)}) %all-to-all-start.7) | async-done | bytes 491552 | tf_op jit(solution)/shard_map/all_to_all | solution.py:48
  603.2 9.5 %all-to-all-done.9 = bf16[1,10,96,256]{3,1,0,2:T(8,128)(2,1)S(1)} async-done(((bf16[1,10,96,256]{3,1,0,2:T(8,128)(2,1)}), bf16[1,10,96,256]{3,1,0,2:T(8,128)(2,1)S(1)}, u32[]{:S(2)}, u32[]{:S(2)}) %all-to-all-start.9) | async-done | bytes 491552 | tf_op jit(solution)/shard_map/all_to_all | solution.py:48
  (206 shorter events, 177.5 us)
Async XLA Ops:
  6.5 177.3 %copy-start = (bf16[8,256,768]{2,1,0:T(8,128)(2,1)S(1)}, bf16[8,256,768]{2,1,0:T(8,128)(2,1)}, u32[]{:S(2)}) copy-start(bf16[8,256,768]{2,1,0:T(8,128)(2,1)} %param.8) | copy-start | bytes 9437188
  14.3 20.8 %copy-start.13 = (s32[384]{0:T(512)}, s32[384]{0:T(512)S(1)}, u32[]{:S(2)}) copy-start(s32[384]{0:T(512)S(1)} %eq.172) | copy-start | bytes 4612
  20.0 0.8 copy-start.8
  23.5 18.8 %copy-start.14 = (s32[384]{0:T(512)}, s32[384]{0:T(512)S(1)}, u32[]{:S(2)}) copy-start(s32[384]{0:T(512)S(1)} %eq.176) | copy-start | bytes 4612
  32.6 9.6 %copy-start.15 = (s32[384]{0:T(512)}, s32[384]{0:T(512)S(1)}, u32[]{:S(2)}) copy-start(s32[384]{0:T(512)S(1)} %eq.180) | copy-start | bytes 4612
  38.3 0.8 copy-start.10
  73.1 26.4 %copy-start.16 = (s32[160]{0:T(256)S(1)}, s32[160]{0:T(256)}, u32[]{:S(2)}) copy-start(s32[160]{0:T(256)} %param.9) | copy-start | bytes 1924
  82.4 40.9 %all-to-all-start = ((bf16[16,10,6,256]{3,2,1,0:T(8,128)(2,1)}), bf16[16,10,6,256]{3,2,1,0:T(8,128)(2,1)}, u32[]{:S(2)}, u32[]{:S(2)}) async-start(bf16[16,10,6,256]{3,2,1,0:T(8,128)(2,1)} %broadcast_select_fusion.5), calls=%async_computation | async-start | bytes 1310720 | tf_op jit(solution)/shard_map/all_to_all | solution.py:36
  123.3 19.7 %all-to-all-start.4 = ((bf16[16,10,6,256]{3,2,1,0:T(8,128)(2,1)}), bf16[16,10,6,256]{3,2,1,0:T(8,128)(2,1)}, u32[]{:S(2)}, u32[]{:S(2)}) async-start(bf16[16,10,6,256]{3,2,1,0:T(8,128)(2,1)} %broadcast_select_fusion.4), calls=%async_computation.4 | async-start | bytes 1310720 | tf_op jit(solution)/shard_map/all_to_all | solution.py:36
  143.0 15.9 %all-to-all-start.6 = ((bf16[16,10,6,256]{3,2,1,0:T(8,128)(2,1)}), bf16[16,10,6,256]{3,2,1,0:T(8,128)(2,1)}, u32[]{:S(2)}, u32[]{:S(2)}) async-start(bf16[16,10,6,256]{3,2,1,0:T(8,128)(2,1)} %broadcast_select_fusion.3), calls=%async_computation.6 | async-start | bytes 1310720 | tf_op jit(solution)/shard_map/all_to_all | solution.py:36
  158.9 18.2 %all-to-all-start.8 = ((bf16[16,10,6,256]{3,2,1,0:T(8,128)(2,1)}), bf16[16,10,6,256]{3,2,1,0:T(8,128)(2,1)}, u32[]{:S(2)}, u32[]{:S(2)}) async-start(bf16[16,10,6,256]{3,2,1,0:T(8,128)(2,1)} %broadcast_select_fusion.2), calls=%async_computation.8 | async-start | bytes 1310720 | tf_op jit(solution)/shard_map/all_to_all | solution.py:36
  177.0 187.4 %all-to-all-start.1 = ((bf16[16,256,1536]{2,1,0:T(8,128)(2,1)}), bf16[16,256,1536]{2,1,0:T(8,128)(2,1)}, u32[]{:S(2)}, u32[]{:S(2)}) async-start(bf16[16,256,1536]{2,1,0:T(8,128)(2,1)} %broadcast_select_fusion), calls=%async_computation.1 | async-start | bytes 25165824 | tf_op jit(solution)/shard_map/all_to_all | solution.py:77
  364.4 89.3 %all-to-all-start.2 = ((bf16[16,256,768]{2,1,0:T(8,128)(2,1)}), bf16[16,256,768]{2,1,0:T(8,128)(2,1)}, u32[]{:S(2)}, u32[]{:S(2)}) async-start(bf16[16,256,768]{2,1,0:T(8,128)(2,1)} %broadcast_select_fusion.1), calls=%async_computation.2 | async-start | bytes 12582912 | tf_op jit(solution)/shard_map/all_to_all | solution.py:78
  369.4 160.9 %all-reduce.3.cloned.1.call-start = ((), (), s32[]{:S(2)}) async-start(), calls=%async_computation.10 | async-start | bytes 23592960 | tf_op jit(solution)/shard_map/psum | solution.py:40
  379.2 6.4 %copy-start.2 = (bf16[10,256,1536]{2,1,0:T(8,128)(2,1)S(1)}, bf16[10,256,1536]{2,1,0:T(8,128)(2,1)}, u32[]{:S(2)}) copy-start(bf16[10,256,1536]{2,1,0:T(8,128)(2,1)} %gather_fusion.2) | copy-start | bytes 23592964
  530.3 3.0 copy-start.3
  535.9 23.7 %all-to-all-start.3 = ((bf16[1,10,96,256]{3,1,0,2:T(8,128)(2,1)}), bf16[1,10,96,256]{3,1,0,2:T(8,128)(2,1)S(1)}, u32[]{:S(2)}, u32[]{:S(2)}) async-start(bf16[1,10,96,256]{3,1,0,2:T(8,128)(2,1)} %copy.116), calls=%async_computation.3 | async-start | bytes 1572864 | tf_op jit(solution)/shard_map/all_to_all | solution.py:48
  543.0 3.0 copy-start.4
  546.0 2.6 copy-start.6
  559.5 18.7 %all-to-all-start.5 = ((bf16[1,10,96,256]{3,1,0,2:T(8,128)(2,1)}), bf16[1,10,96,256]{3,1,0,2:T(8,128)(2,1)S(1)}, u32[]{:S(2)}, u32[]{:S(2)}) async-start(bf16[1,10,96,256]{3,1,0,2:T(8,128)(2,1)} %copy.125), calls=%async_computation.5 | async-start | bytes 1572864 | tf_op jit(solution)/shard_map/all_to_all | solution.py:48
  563.4 6.6 %copy-start.5 = (bf16[10,96,1536]{2,1,0:T(8,128)(2,1)S(1)}, bf16[10,96,1536]{2,1,0:T(8,128)(2,1)}, u32[]{:S(2)}) copy-start(bf16[10,96,1536]{2,1,0:T(8,128)(2,1)} %get-tuple-element.39) | copy-start | bytes 8847364
  578.3 17.5 %all-to-all-start.7 = ((bf16[1,10,96,256]{3,1,0,2:T(8,128)(2,1)}), bf16[1,10,96,256]{3,1,0,2:T(8,128)(2,1)S(1)}, u32[]{:S(2)}, u32[]{:S(2)}) async-start(bf16[1,10,96,256]{3,1,0,2:T(8,128)(2,1)} %copy.134), calls=%async_computation.7 | async-start | bytes 1572864 | tf_op jit(solution)/shard_map/all_to_all | solution.py:48
  595.7 17.0 %all-to-all-start.9 = ((bf16[1,10,96,256]{3,1,0,2:T(8,128)(2,1)}), bf16[1,10,96,256]{3,1,0,2:T(8,128)(2,1)S(1)}, u32[]{:S(2)}, u32[]{:S(2)}) async-start(bf16[1,10,96,256]{3,1,0,2:T(8,128)(2,1)} %copy.143), calls=%async_computation.9 | async-start | bytes 1572864 | tf_op jit(solution)/shard_map/all_to_all | solution.py:48
  613.8 14.7 %copy-start.1 = (bf16[8,256,768]{2,1,0:T(8,128)(2,1)S(1)}, bf16[8,256,768]{2,1,0:T(8,128)(2,1)}, u32[]{:S(2)}) copy-start(bf16[8,256,768]{2,1,0:T(8,128)(2,1)} %param.8) | copy-start | bytes 9437188
  (4 other events, 2.9 us)
Sparse Core Ops, SparseCore 0:
  394.7 135.4 all-reduce.2
where the time goes:
time: 647 us; the launch traced here: 636 us
  waiting for transfers between devices  335 us (52%)
  local copies, waits for them, and re-layouts  148 us (23%)
  starting transfers between devices  56.7 us (9%)
  other arithmetic  52.6 us (8%)
  matrix products  28.8 us (4%)
  between operations  14.6 us (2%)
    all_to_all x1, waiting for transfers between devices, local(): lax.all_to_all(chosen_in, 'ep', split_axis=0, concat_axis=0, tiled=True)  166 us
    psum x1, waiting for transfers between devices, decode(): summed = lax.psum(partial_value, 'fsdp').astype(jnp.float32)  70.8 us
    all_to_all x1, waiting for transfers between devices, local(): lax.all_to_all(chosen_out, 'ep', split_axis=0, concat_axis=0, tiled=True)  58.4 us
    another operation x36, local copies, waits for them, and re-layouts  44.4 us
    all_to_all x4, waiting for transfers between devices, decode(): lax.all_to_all(result[None], 'ep', split_axis=2, concat_axis=0, tiled=True)  29.4 us
    gather x8, local copies, waits for them, and re-layouts, decode(): features[source]  27.9 us
    all_to_all x4, starting transfers between devices, decode(): lax.all_to_all(outgoing, 'ep', split_axis=0, concat_axis=2, tiled=True)[0]  26.5 us
    all_to_all x4, starting transfers between devices, decode(): lax.all_to_all(result[None], 'ep', split_axis=2, concat_axis=0, tiled=True)  18.2 us
  transfers between devices with their start and end apart: 11, of which 10 were waited for; matrix products, arithmetic and copies ran while one was open for 21% of the time, Pallas kernels for 0%

commit v1 on v0

v1 whole, which is shorter than its diff:
```python
import functools

import jax
import jax.numpy as jnp
from jax import lax
from jax.experimental import pallas as pl
from jax.experimental.pallas import tpu as pltpu
from jax.sharding import PartitionSpec as P

CAP = 2304
TILE = 256
LANES = 512
ALIGN = 16
I32, F32, BF16 = jnp.int32, jnp.float32, jnp.bfloat16


def select_rows(pos, val, offs, first, last, base, lane, tile):
    slot = lax.broadcasted_iota(I32, (tile, LANES), 0)

    def one(e, block):
        where = pos[pl.ds(e, 1), pl.ds(lane, LANES)] - base
        value = 1.0 if val is None else val[pl.ds(e, 1), pl.ds(lane, LANES)]
        return jnp.where(where == slot, value, block)

    return lax.fori_loop(first, last, one, jnp.zeros((tile, LANES), F32)).astype(BF16)


def overlap(offs, base, tile, experts):
    first = jnp.int32(0)
    last = jnp.int32(0)
    for e in range(experts):
        first += jnp.where(offs[e + 1] <= base, 1, 0)
        last += jnp.where(offs[e] < base + tile, 1, 0)
    return first, last


def spread(me, base, codes, tokens, weights, part, pos, val, offs, wbuf, sems, xbuf, pbuf, osem):
    experts = weights.shape[0]
    rows = tokens.shape[0]
    loads = [pltpu.make_async_copy(weights.at[e], wbuf.at[e], sems.at[e]) for e in range(experts)]
    for load in loads:
        load.start()
    tri = (
        lax.broadcasted_iota(I32, (256, 256), 0) < lax.broadcasted_iota(I32, (256, 256), 1)
    ).astype(BF16)
    carry = jnp.zeros((experts, 1), F32)
    for c in range(rows // 256):
        span = slice(c * 256, (c + 1) * 256)
        code = codes[:, span]
        local = (code >> 4) - me[0] * experts
        gates = (code & 15).astype(F32)
        total = jnp.concatenate(
            [
                jnp.sum(jnp.where(local == e, gates, 0.0), axis=0, keepdims=True)
                for e in range(experts)
            ],
            axis=0,
        )
        chosen = (total > 0).astype(F32)
        before = jnp.dot(chosen.astype(BF16), tri, preferred_element_type=F32) + carry
        carry = carry + jnp.sum(chosen, axis=1, keepdims=True)
        val[:, span] = total
        pos[:, span] = jnp.where(total > 0, before, -1e6).astype(I32)
    row_of = lax.broadcasted_iota(I32, (experts, 1), 0)
    total = jnp.int32(0)
    starts = jnp.zeros((experts, 1), I32)
    for e in range(experts):
        count = jnp.sum(jnp.where(row_of == e, carry, 0.0)).astype(I32)
        offs[e] = total
        starts = jnp.where(row_of == e, total, starts)
        total += (count + ALIGN - 1) // ALIGN * ALIGN
    offs[experts] = total
    pos[...] += starts - base[0]

    def gather(j, _):
        at = pl.multiple_of(j * TILE, TILE)
        first, last = overlap(offs, at + base[0], TILE, experts)

        def lanes(c, x):
            lane = pl.multiple_of(c * LANES, LANES)
            hot = select_rows(pos, None, offs, first, last, at, lane, TILE)
            return x + jnp.dot(hot, tokens[pl.ds(lane, LANES), :], preferred_element_type=F32)

        x = lax.fori_loop(
            0, rows // LANES, lanes, jnp.zeros((TILE, tokens.shape[1]), F32)
        )
        xbuf[pl.ds(at, TILE), :] = x.astype(BF16)
        return 0

    lax.fori_loop(0, CAP // TILE, gather, 0)
    xbuf[CAP:, :] = jnp.zeros((TILE, tokens.shape[1]), BF16)

    def group(e, _):
        pltpu.make_async_copy(weights.at[e], wbuf.at[e], sems.at[e]).wait()
        low = jnp.clip(offs[e] - base[0], 0, CAP)
        high = jnp.clip(offs[e + 1] - base[0], 0, CAP)

        def tile(i, _):
            at = pl.multiple_of(low + i * TILE, ALIGN)
            pbuf[pl.ds(at, TILE), :] = jnp.dot(
                xbuf[pl.ds(at, TILE), :], wbuf[e], preferred_element_type=F32
            ).astype(BF16)
            return 0

        return lax.fori_loop(0, (high - low + TILE - 1) // TILE, tile, 0)

    lax.fori_loop(0, experts, group, 0)
    end = jnp.clip(offs[experts] - base[0], 0, CAP)

    def clear(i, _):
        at = pl.multiple_of(end + i * ALIGN, ALIGN)
        pbuf[pl.ds(at, ALIGN), :] = jnp.zeros((ALIGN, pbuf.shape[1]), BF16)
        return 0

    lax.fori_loop(0, (CAP - end) // ALIGN, clear, 0)
    out = pltpu.make_async_copy(pbuf.at[pl.ds(0, CAP)], part, osem)
    out.start()
    out.wait()


def call_spread(me, base, codes, tokens, weights):
    experts, depth, width = weights.shape
    rows = tokens.shape[0]
    smem = pl.BlockSpec(memory_space=pltpu.SMEM)
    vmem = pl.BlockSpec(memory_space=pltpu.VMEM)
    hbm = pl.BlockSpec(memory_space=pl.ANY)
    return pl.pallas_call(
        spread,
        out_shape=(
            jax.ShapeDtypeStruct((CAP, width), BF16),
            jax.ShapeDtypeStruct((experts, rows), I32),
            jax.ShapeDtypeStruct((experts, rows), F32),
            jax.ShapeDtypeStruct((16,), I32),
        ),
        in_specs=[smem, smem, vmem, vmem, hbm],
        out_specs=(hbm, vmem, vmem, smem),
        scratch_shapes=[
            pltpu.VMEM(weights.shape, BF16),
            pltpu.SemaphoreType.DMA((experts,)),
            pltpu.VMEM((CAP + TILE, depth), BF16),
            pltpu.VMEM((CAP + TILE, width), BF16),
            pltpu.SemaphoreType.DMA,
        ],
        compiler_params=pltpu.CompilerParams(vmem_limit_bytes=48 << 20),
        name="spread",
    )(me, base, codes, tokens, weights)


def collect(base, offs, pos, val, hidden, weights, out, wbuf, sems, rbuf, acc):
    experts = weights.shape[0]
    rows = pos.shape[1]
    depth = weights.shape[1]
    for e in range(experts):
        pltpu.make_async_copy(weights.at[e], wbuf.at[e], sems.at[e]).start()

    def group(e, _):
        pltpu.make_async_copy(weights.at[e], wbuf.at[e], sems.at[e]).wait()
        low = jnp.clip(offs[e] - base[0], 0, CAP)
        high = jnp.clip(offs[e + 1] - base[0], 0, CAP)

        def tile(i, _):
            at = pl.multiple_of(jnp.minimum(low + i * TILE, CAP - TILE), ALIGN)
            block = lax.dot_general(
                hidden[pl.ds(at, TILE), :],
                wbuf[e],
                (((1,), (1,)), ((), ())),
                preferred_element_type=F32,
            ).astype(BF16)
            inside = lax.broadcasted_iota(I32, (TILE, 1), 0) + at >= low
            rbuf[pl.ds(at, TILE), :] = jnp.where(inside, block, rbuf[pl.ds(at, TILE), :])
            return 0

        return lax.fori_loop(0, (high - low + TILE - 1) // TILE, tile, 0)

    rbuf[...] = jnp.zeros_like(rbuf)
    lax.fori_loop(0, experts, group, 0)
    acc[...] = jnp.zeros_like(acc)

    def combine(j, _):
        at = pl.multiple_of(j * TILE, TILE)
        first, last = overlap(offs, at + base[0], TILE, experts)

        def lanes(c, _):
            lane = pl.multiple_of(c * LANES, LANES)
            hot = select_rows(pos, val, offs, first, last, at, lane, TILE)
            acc[:, pl.ds(lane, LANES)] += lax.dot_general(
                rbuf[pl.ds(at, TILE), :],
                hot,
                (((0,), (0,)), ((), ())),
                preferred_element_type=F32,
            )
            return 0

        return lax.fori_loop(0, rows // LANES, lanes, 0)

    lax.fori_loop(0, CAP // TILE, combine, 0)

    def flip(c, _):
        lane = pl.multiple_of(c * 256, 256)
        out[pl.ds(lane, 256), :] = acc[:, pl.ds(lane, 256)].T.astype(out.dtype)
        return 0

    lax.fori_loop(0, rows // 256, flip, 0)


def call_collect(base, offs, pos, val, hidden, weights):
    experts, depth, width = weights.shape
    rows = pos.shape[1]
    smem = pl.BlockSpec(memory_space=pltpu.SMEM)
    vmem = pl.BlockSpec(memory_space=pltpu.VMEM)
    hbm = pl.BlockSpec(memory_space=pl.ANY)
    return pl.pallas_call(
        collect,
        out_shape=jax.ShapeDtypeStruct((rows, depth), BF16),
        in_specs=[smem, smem, vmem, vmem, vmem, hbm],
        out_specs=vmem,
        scratch_shapes=[
            pltpu.VMEM(weights.shape, BF16),
            pltpu.SemaphoreType.DMA((experts,)),
            pltpu.VMEM((CAP, depth), BF16),
            pltpu.VMEM((depth, rows), F32),
        ],
        compiler_params=pltpu.CompilerParams(vmem_limit_bytes=48 << 20),
        name="collect",
    )(base, offs, pos, val, hidden, weights)


def local(tokens, gate_up_weight, down_weight, placement, copy_ids, gate_codes):
    steps, rows, depth = tokens.shape
    experts, units = gate_up_weight.shape[0], down_weight.shape[2]
    top = copy_ids.shape[2]
    own = lax.axis_index("ep").astype(I32).reshape(1)
    ids = copy_ids.reshape(steps * rows, top).T
    hot = ids[:, :, None] == jnp.arange(placement.shape[0], dtype=I32)
    expert = jnp.sum(jnp.where(hot, placement, 0), axis=2)
    packed = expert * 16 + gate_codes.reshape(steps * rows, top).T
    codes = lax.all_gather(packed, "ep", axis=1, tiled=True)
    everyone = lax.all_gather(tokens.reshape(steps * rows, depth), "ep", axis=0, tiled=True)
    tally = jnp.sum(
        (codes.reshape(-1) >> 4)[None, :] == jnp.arange(experts * lax.axis_size("ep"), dtype=I32)[:, None],
        axis=1,
        dtype=I32,
    )
    most = jnp.max(jnp.sum(((tally + ALIGN - 1) // ALIGN * ALIGN).reshape(-1, experts), axis=1))

    def chunk(at):
        base = (at * CAP).reshape(1)
        part, pos, val, offs = call_spread(own, base, codes, everyone, gate_up_weight)
        summed = lax.psum_scatter(part, "fsdp", scatter_dimension=0, tiled=True).astype(F32)
        hidden = (jax.nn.silu(summed[:, :units]) * summed[:, units:]).astype(BF16)
        hidden = lax.all_gather(hidden, "fsdp", axis=0, tiled=True)
        return call_collect(base, offs, pos, val, hidden, down_weight)

    mixed = chunk(jnp.int32(0))
    _, mixed = lax.while_loop(
        lambda c: c[0] * CAP < most,
        lambda c: (c[0] + 1, (c[1].astype(F32) + chunk(c[0]).astype(F32)).astype(BF16)),
        (jnp.int32(1), mixed),
    )
    mixed = lax.psum_scatter(mixed, "ep", scatter_dimension=0, tiled=True).astype(F32)
    total = jnp.sum(gate_codes, axis=2).astype(F32)
    return (mixed.reshape(steps, rows, depth) / total[:, :, None]).astype(BF16)


def solution(mesh):
    in_specs = (
        P(None, "ep", "fsdp"),
        P("ep", "fsdp", None),
        P("ep", "fsdp", None),
        P(),
        P(None, "ep", None),
        P(None, "ep", None),
    )
    out_specs = P(None, "ep", "fsdp")
    return jax.shard_map(local, mesh=mesh, in_specs=in_specs, out_specs=out_specs, check_vma=False)
```

time: 647 us -> 301 us (0.47); the launches traced: 636 us -> 302 us
  waiting for transfers between devices: 335 us -> 175 us
  local copies, waits for them, and re-layouts: 148 us -> 3.87 us
  Pallas kernels: 0 us -> 77.5 us
  starting transfers between devices: 56.7 us -> 0.13 us
  other arithmetic: 52.6 us -> 7.12 us
  matrix products: 28.8 us -> 0 us
  blocking collectives: 0 us -> 25.1 us
    all_to_all x10 -> x0, waiting for transfers between devices: 264 us -> none  [the longest x1 166 us: local(): lax.all_to_all(chosen_in, 'ep', split_axis=0, concat_axis=0, tiled=True)]
    reduce_scatter x0 -> x2, waiting for transfers between devices: none -> 125 us  [the longest x1 80.3 us: local(): lax.psum_scatter(mixed, 'ep', scatter_dimension=0, tiled=True).astype(F32)]
    pallas_call x0 -> x2, Pallas kernels: none -> 77.5 us  [the longest x1 39.5 us: call_spread(): pl.pallas_call(spread, out_shape=(jax.ShapeDtypeStruct((CAP, width), BF16...]
    psum x1 -> x0, waiting for transfers between devices: 70.8 us -> none  [decode(): summed = lax.psum(partial_value, 'fsdp').astype(jnp.float32)]
    gather x16 -> x0, local copies, waits for them, and re-layouts: 67 us -> none  [the longest x8 27.9 us: decode(): features[source]]
    all_to_all x10 -> x0, starting transfers between devices: 56.5 us -> none  [the longest x4 26.5 us: decode(): lax.all_to_all(outgoing, 'ep', split_axis=0, concat_axis=2, tiled=True)[0]]
    all_gather x0 -> x2, waiting for transfers between devices: none -> 48.5 us  [the longest x1 27.9 us: chunk(): hidden = lax.all_gather(hidden, 'fsdp', axis=0, tiled=True)]
    another operation x36 -> x0, local copies, waits for them, and re-layouts: 44.4 us -> none
  transfers between devices with their start and end apart: 11 -> 4, of which waited for: 10 -> 4; matrix products, arithmetic and copies ran while one was open for 21% -> 2% of each run, Pallas kernels for 0% -> 0%
where the time goes in v1:
time: 301 us; the launch traced here: 302 us
  waiting for transfers between devices  175 us (58%)
  Pallas kernels  77.5 us (26%)
  blocking collectives  25.1 us (8%)
  between operations  13.2 us (4%)
  other arithmetic  7.12 us (2%)
  local copies, waits for them, and re-layouts  3.87 us (1%)
    reduce_scatter x1, waiting for transfers between devices, local(): lax.psum_scatter(mixed, 'ep', scatter_dimension=0, tiled=True).astype(F32)  80.3 us
    reduce_scatter x1, waiting for transfers between devices, chunk(): lax.psum_scatter(part, 'fsdp', scatter_dimension=0, tiled=True).astype(F32)  44.7 us
    pallas_call x1, Pallas kernels, call_spread(): pl.pallas_call(spread, out_shape=(jax.ShapeDtypeStruct((CAP, width), BF16...  39.5 us
    pallas_call x1, Pallas kernels, call_collect(): pl.pallas_call(collect, out_shape=jax.ShapeDtypeStruct((rows, depth), BF1...  38 us
    all_gather x1, waiting for transfers between devices, chunk(): hidden = lax.all_gather(hidden, 'fsdp', axis=0, tiled=True)  27.9 us
    all_gather x1, blocking collectives, local(): codes = lax.all_gather(packed, 'ep', axis=1, tiled=True)  25.1 us
    all_gather x1, waiting for transfers between devices, local(): lax.all_gather(tokens.reshape(steps * rows, depth), 'ep', axis=0, tiled=T...  20.6 us
  transfers between devices with their start and end apart: 4, of which 4 were waited for; matrix products, arithmetic and copies ran while one was open for 2% of the time, Pallas kernels for 0%

profile of v1, /device:TPU:8, one launch (start us, length us, event | category | flops | bytes accessed | tf_op | source)
XLA Modules:
  0.0 302.3 jit_solution(18332870688171548418)
XLA Ops:
  6.5 0.7 all-gather.5.cloned.1.call-update
  7.3 0.7 copy.15
  8.0 0.1 reshape.39
  8.1 0.7 copy.14
  8.8 0.1 reshape.38
  8.9 1.0 select_reduce_fusion
  9.9 25.1 %all-gather = s32[16,192,8]{1,2,0:T(8,128)S(1)} all-gather(s32[1,192,8]{1,2,0:T(8,128)S(1)} %fusion.6), channel_id=1, replica_groups=mesh['ep'=16,'fsdp'=8] {'ep'}, dimensions={0}, use_global_device_ids=true | all-gather | bytes 104448 | tf_op jit(solution)/shard_map/all_gather | solution.py:237
  35.0 0.1 reshape.46
  35.1 20.6 %all-gather.5.cloned.1.call-done.tokens = bf16[3072,256]{1,0:T(8,128)(2,1)} async-done(((bf16[192,256]{1,0:T(8,128)(2,1)}), bf16[3072,256]{1,0:T(8,128)(2,1)}) %all-gather.5.cloned.1.call-update) | async-done | bytes 1572880 | tf_op jit(solution)/shard_map/all_gather | solution.py:238
  55.7 39.5 %spread.2 = (bf16[2304,1536]{1,0:T(8,128)(2,1)}, s32[8,3072]{1,0:T(8,128)S(1)}, f32[8,3072]{1,0:T(8,128)S(1)}, s32[16]{0:T(128)S(1)}) custom-call(s32[1]{0:T(128)} %bitcast.1.me, s32[1]{0:T(128)} %constant.37.clone.1.base, s32[8,3072]{1,0:T(8,128)S(1)} %bitcast.27, bf16[3072,256]{1,0:T(8,128)(2,1)} %all-gather.5.cloned.1.call-done.tokens, ...), custom_call_target="tpu_custom_call" | custom-call | tf_op jit(solution)/shard_map/spread/pallas_call | solution.py:127
  95.3 44.7 %reduce-scatter.4.cloned.1.call-done = bf16[288,1536]{1,0:T(8,128)(2,1)} async-done(((bf16[2304,1536]{1,0:T(8,128)(2,1)}), bf16[288,1536]{1,0:T(8,128)(2,1)}) %reduce-scatter.4.cloned.1.call-update) | async-done | bytes 884752 | tf_op jit(solution)/shard_map/reduce_scatter | solution.py:249
  140.0 1.4 convert_element_type.35
  141.4 1.0 fusion.1
  142.5 1.3 convert_reduce_fusion
  143.8 0.1 sub.18
  143.9 0.1 fusion.5
  144.0 0.7 reduce_max.9
  144.7 27.9 %all-gather.7.cloned.1.call-done.hidden = bf16[2304,768]{1,0:T(8,128)(2,1)} async-done(((bf16[288,768]{1,0:T(8,128)(2,1)}), bf16[2304,768]{1,0:T(8,128)(2,1)}) %all-gather.7.cloned.1.call-update) | async-done | bytes 3538960 | tf_op jit(solution)/shard_map/all_gather | solution.py:251
  172.6 2.0 copy-done.1
  174.6 38.0 %collect.2 = bf16[3072,256]{1,0:T(8,128)(2,1)} custom-call(s32[1]{0:T(128)} %constant.37.clone.1.base, s32[16]{0:T(128)S(1)} %get-tuple-element.56.offs, s32[8,3072]{1,0:T(8,128)S(1)} %get-tuple-element.57.pos, f32[8,3072]{1,0:T(8,128)S(1)} %get-tuple-element.58.val, bf16[2304,768]{1,0:T(8,128)(2,1)S(1)} %copy-done.1, bf16[8,256,768]{2,1,0:T(8,128)(2,1)S(1)} %copy-done.2), custom_call_target="tpu_custom_call" | custom-call | tf_op jit(solution)/shard_map/collect/pallas_call | solution.py:212
  212.6 0.7 while.10
  213.3 0.5 reduce-scatter.6.cloned.1.call-update
  213.9 80.3 %reduce-scatter.6.cloned.1.call-done = bf16[192,256]{1,0:T(8,128)(2,1)} async-done(((bf16[3072,256]{1,0:T(8,128)(2,1)}), bf16[192,256]{1,0:T(8,128)(2,1)}) %reduce-scatter.6.cloned.1.call-update) | async-done | bytes 98320 | tf_op jit(solution)/shard_map/reduce_scatter | solution.py:260
  294.2 1.6 fusion.2
  (18 shorter events, 0.3 us)
Async XLA Ops:
  6.5 49.1 %all-gather.5.cloned.1.call-start = ((), (), s32[]{:S(2)}) async-start(), calls=%async_computation.3 | async-start | bytes 1671168 | tf_op jit(solution)/shard_map/all_gather | solution.py:238
  7.3 132.8 %reduce-scatter.4.cloned.1.call-start = ((), (), s32[]{:S(2)}) async-start(), calls=%async_computation.4 | async-start | bytes 7962624 | tf_op jit(solution)/shard_map/reduce_scatter | solution.py:249
  95.2 77.4 %all-gather.7.cloned.1.call-start = ((), (), s32[]{:S(2)}) async-start(), calls=%async_computation.5 | async-start | bytes 3981312 | tf_op jit(solution)/shard_map/all_gather | solution.py:251
  141.4 31.2 %copy-start.2 = (bf16[8,256,768]{2,1,0:T(8,128)(2,1)S(1)}, bf16[8,256,768]{2,1,0:T(8,128)(2,1)}, u32[]{:S(2)}) copy-start(bf16[8,256,768]{2,1,0:T(8,128)(2,1)} %weights.3) | copy-start | bytes 9437188
  172.6 2.0 copy-start.1
  212.6 1.3 copy-start.5
  213.3 80.9 %reduce-scatter.6.cloned.1.call-start = ((), (), s32[]{:S(2)}) async-start(), calls=%async_computation.6 | async-start | bytes 1671168 | tf_op jit(solution)/shard_map/reduce_scatter | solution.py:260
Sparse Core Ops, SparseCore 0:
  9.5 46.1 all-gather.4
  95.4 44.6 reduce-scatter.3
  142.6 30.0 all-gather.6
  217.0 77.1 reduce-scatter.5

commit v2 on v1

v2 whole, which is shorter than its diff:
```python
import functools

import jax
import jax.numpy as jnp
from jax import lax
from jax.experimental import pallas as pl
from jax.experimental.pallas import tpu as pltpu
from jax.sharding import PartitionSpec as P

I32, F32, BF16 = jnp.int32, jnp.float32, jnp.bfloat16
CAP = 2304
TILE = 256
LANES = 512
ALIGN = 16
WAVES = 6
MESH = pl.DeviceIdType.MESH
SIDE = 4
LOW, HIGH = 0, 1


class Post:
    def __init__(self, sends, recvs):
        self.sends, self.recvs, self.made = sends, recvs, {}

    def send(self, key, src, dst, target):
        number = self.made.setdefault(key, len(self.made))
        copy = pltpu.make_async_remote_copy(
            src_ref=src,
            dst_ref=dst,
            send_sem=self.sends.at[number],
            recv_sem=self.recvs.at[number],
            device_id=target,
            device_id_type=MESH,
        )
        copy.start()
        self.made[key] = number
        setattr(self, "copy_%d" % number, copy)

    def arrived(self, key):
        getattr(self, "copy_%d" % self.made[key]).wait_recv()

    def drain(self):
        for number in self.made.values():
            getattr(self, "copy_%d" % number).wait_send()


def greet(targets):
    barrier = pltpu.get_barrier_semaphore()
    for target in targets:
        pl.semaphore_signal(barrier, inc=1, device_id=target, device_id_type=MESH)
    pl.semaphore_wait(barrier, len(targets))


def torus():
    me = lax.axis_index("ep")
    z, x = lax.div(me, SIDE), lax.rem(me, SIDE)

    def at(dz, dx):
        return lax.rem(z + dz, SIDE) * SIDE + lax.rem(x + dx, SIDE)

    return me, z, x, at


def share(codes, tokens, codes_all, tokens_all, keep, csend, crecv, sends, recvs):
    me, z, x, at = torus()
    greet([{"ep": lax.rem(me + d, SIDE * SIDE)} for d in range(1, SIDE * SIDE)])
    rows, depth = tokens.shape
    half = depth // 2
    near = []
    for d in range(1, SIDE * SIDE):
        copy = pltpu.make_async_remote_copy(
            src_ref=codes,
            dst_ref=codes_all.at[me],
            send_sem=csend.at[d],
            recv_sem=crecv.at[d],
            device_id={"ep": lax.rem(me + d, SIDE * SIDE)},
            device_id_type=MESH,
        )
        copy.start()
        near.append(copy)
    post = Post(sends, recvs)
    mine = pltpu.make_async_copy(tokens, tokens_all.at[me], keep.at[0])
    mine.start()
    mine_codes = pltpu.make_async_copy(codes, codes_all.at[me], keep.at[1])
    mine_codes.start()

    def place(side, first, second):
        return at(second, first) if side == 0 else at(first, second)

    def block(side, first, second, part=None):
        span = slice(None) if part is None else pl.ds(part * (rows // 2), rows // 2)
        return tokens_all.at[place(side, first, second), span, pl.ds(side * half, half)]

    def target(side, axis, step):
        first, second = (step, 0) if axis == 1 else (0, step)
        return {"ep": place(side, first, second)}

    for axis in (1, 2):
        for side in (0, 1):
            own = tokens.at[:, pl.ds(side * half, half)]
            for step in (1, 3):
                post.send((side, axis, 0, step), own, block(side, 0, 0), target(side, axis, step))

    def onward(side, first):
        src = block(side, first, 0)
        for step in (1, 3):
            post.send((side, 2, first, step), src, src, target(side, 2, step))

    for step in (1, 3):
        for side in (0, 1):
            post.arrived((side, 1, 0, step))
            part = LOW if step == 1 else HIGH
            src = block(side, 4 - step, 0, part)
            post.send((side, 1, "far", step), src, src, target(side, 1, step))
            onward(side, 4 - step)

    def relay(side, first):
        for step in (1, 3):
            post.arrived((side, 2, first, step))
            part = LOW if step == 1 else HIGH
            src = block(side, first, 4 - step, part)
            post.send((side, 2, first, "far", step), src, src, target(side, 2, step))

    for side in (0, 1):
        relay(side, 0)
    for side in (0, 1):
        for step in (1, 3):
            post.arrived((side, 1, "far", step))
        onward(side, 2)
    for first in (3, 1, 2):
        for side in (0, 1):
            relay(side, first)
    for first in (0, 3, 1, 2):
        for side in (0, 1):
            for step in (1, 3):
                post.arrived((side, 2, first, "far", step))
    for copy in near:
        copy.wait()
    post.drain()
    mine.wait()
    mine_codes.wait()


def call_share(codes, tokens):
    peers = SIDE * SIDE
    vmem = pl.BlockSpec(memory_space=pltpu.VMEM)
    hbm = pl.BlockSpec(memory_space=pl.ANY)
    return pl.pallas_call(
        share,
        out_shape=(
            jax.ShapeDtypeStruct((peers,) + codes.shape, codes.dtype),
            jax.ShapeDtypeStruct((peers,) + tokens.shape, tokens.dtype),
        ),
        in_specs=[vmem, vmem],
        out_specs=(hbm, hbm),
        scratch_shapes=[
            pltpu.SemaphoreType.DMA((2,)),
            pltpu.SemaphoreType.DMA((peers,)),
            pltpu.SemaphoreType.DMA((peers,)),
            pltpu.SemaphoreType.DMA((40,)),
            pltpu.SemaphoreType.DMA((40,)),
        ],
        compiler_params=pltpu.CompilerParams(collective_id=1, has_side_effects=True),
        name="share",
    )(codes, tokens)


def settle(parts, out, big, mid, small, tiny, sends, recvs):
    me, z, x, at = torus()
    greet([{"ep": at(0, 1)}, {"ep": at(0, 3)}, {"ep": at(1, 0)}, {"ep": at(3, 0)}])
    rows, depth = parts.shape[2:]
    half, lot = depth // 2, rows // 2
    post = Post(sends, recvs)
    axis_one = (x, z)
    axis_two = (z, x)

    def wide(side, step, part):
        to = lax.rem(axis_one[side] + step, SIDE)
        spot = (slice(None), to) if side == 0 else (to, slice(None))
        return parts.at[spot + (pl.ds(part * lot, lot), pl.ds(side * half, half))]

    def target(side, stage, step):
        along_x = (side == 0) == (stage == 1)
        return {"ep": at(0, step) if along_x else at(step, 0)}

    def add(a, b):
        return a[...].astype(F32) + b[...].astype(F32)

    def ring(side, stage, source, slots, fill):
        go = functools.partial(target, side, stage)
        yield
        post.send((side, stage, 0), source(2, LOW), slots.at[0], go(1))
        post.send((side, stage, 1), source(2, HIGH), slots.at[1], go(3))
        yield
        post.send((side, stage, 3), source(1, HIGH), slots.at[3], go(1))
        post.send((side, stage, 2), source(3, LOW), slots.at[2], go(3))
        yield
        post.arrived((side, stage, 0))
        fill[0] = add(source(1, LOW), slots.at[0]).astype(BF16)
        post.send((side, stage, 4), fill.at[0], slots.at[4], go(1))
        post.arrived((side, stage, 1))
        fill[1] = add(source(3, HIGH), slots.at[1]).astype(BF16)
        post.send((side, stage, 5), fill.at[1], slots.at[5], go(3))
        yield
        for slot in (2, 3, 4, 5):
            post.arrived((side, stage, slot))
        yield

    def run(stage, sources, slots, fill):
        rings = [ring(side, stage, sources[side], slots.at[side], fill.at[side]) for side in (0, 1)]
        for _ in range(5):
            for one in rings:
                next(one)

    run(1, [functools.partial(wide, side) for side in (0, 1)], big, mid.at[0])
    sums = mid.at[1]
    for side in (0, 1):
        for part in (LOW, HIGH):
            sums[side, part] = (
                wide(side, 0, part)[...].astype(F32)
                + big[side, 2 + part].astype(F32)
                + big[side, 4 + part].astype(F32)
            ).astype(BF16)

    def narrow(side, step, part):
        return sums.at[side, part, lax.rem(axis_two[side] + step, SIDE)]

    run(2, [functools.partial(narrow, side) for side in (0, 1)], small, tiny)
    for side in (0, 1):
        for part in (LOW, HIGH):
            out[pl.ds(part * lot, lot), pl.ds(side * half, half)] = (
                narrow(side, 0, part)[...].astype(F32)
                + small[side, 2 + part].astype(F32)
                + small[side, 4 + part].astype(F32)
            )
    post.drain()


def call_settle(parts):
    rows, depth = parts.shape[2:]
    lot, half = rows // 2, depth // 2
    vmem = pl.BlockSpec(memory_space=pltpu.VMEM)
    return pl.pallas_call(
        settle,
        out_shape=jax.ShapeDtypeStruct((rows, depth), F32),
        in_specs=[vmem],
        out_specs=vmem,
        scratch_shapes=[
            pltpu.VMEM((2, 6, SIDE, lot, half), BF16),
            pltpu.VMEM((2, 2, 2, SIDE, lot, half), BF16),
            pltpu.VMEM((2, 6, lot, half), BF16),
            pltpu.VMEM((2, 2, lot, half), BF16),
            pltpu.SemaphoreType.DMA((24,)),
            pltpu.SemaphoreType.DMA((24,)),
        ],
        compiler_params=pltpu.CompilerParams(collective_id=2, has_side_effects=True),
        name="settle",
    )(parts)


def blend(waves, part, hidden, own, other, far, direct, summed, fill, made, loads, puts, sends, recvs):
    me = lax.axis_index("fsdp")
    y, core = lax.div(me, 2), lax.rem(me, 2)
    rows = part.shape[3]
    units = part.shape[4] // 2
    partner = {"fsdp": y * 2 + 1 - core}
    sides = {step: {"fsdp": lax.rem(y + step, SIDE) * 2 + core} for step in (1, 3)}
    greet([partner, sides[1], sides[3]])
    post = Post(sends, recvs)

    def chip(step):
        return lax.rem(y + step, SIDE)

    for w in range(waves):
        post.send((w, "swap"), part.at[1 - core, w], other.at[w], partner)
        pltpu.make_async_copy(part.at[core, w], own.at[w], loads.at[w]).start()

    columns = (pl.ds(0, units), pl.ds(units, units))

    def mine(w, step, piece):
        return own.at[w, chip(step), :, columns[piece]]

    def fold(w, step):
        at = chip(step)
        own[w, at] = (own[w, at].astype(F32) + other[w, at].astype(F32)).astype(BF16)

    def first(w):
        pltpu.make_async_copy(part.at[core, w], own.at[w], loads.at[w]).wait()
        post.arrived((w, "swap"))
        fold(w, 2)
        post.send((w, "far", LOW), mine(w, 2, LOW), far.at[w, LOW], sides[1])
        post.send((w, "far", HIGH), mine(w, 2, HIGH), far.at[w, HIGH], sides[3])
        fold(w, 1)
        post.send((w, "direct", HIGH), mine(w, 1, HIGH), direct.at[w, HIGH], sides[1])
        fold(w, 3)
        post.send((w, "direct", LOW), mine(w, 3, LOW), direct.at[w, LOW], sides[3])

    def second(w):
        for piece, step in ((LOW, 1), (HIGH, 3)):
            post.arrived((w, "far", piece))
            fill[w, piece] = (
                mine(w, step, piece)[...].astype(F32) + far[w, piece].astype(F32)
            ).astype(BF16)
            post.send((w, "summed", piece), fill.at[w, piece], summed.at[w, piece], sides[step])

    def third(w):
        fold(w, 0)
        both = []
        for piece in (LOW, HIGH):
            post.arrived((w, "direct", piece))
            post.arrived((w, "summed", piece))
            both.append(
                mine(w, 0, piece)[...].astype(F32)
                + direct[w, piece].astype(F32)
                + summed[w, piece].astype(F32)
            )
        gate, up = both
        made[w] = (gate / (1 + jnp.exp(-gate)) * up).astype(BF16)
        goal = hidden.at[core, w, y]
        for step in (1, 3):
            post.send((w, "round", step), made.at[w], goal, sides[step])
        post.send((w, "cross", 0), made.at[w], goal, partner)
        pltpu.make_async_copy(made.at[w], goal, puts.at[w]).start()

    def fourth(w):
        for step in (1, 3):
            post.arrived((w, "round", step))
            block = hidden.at[core, w, chip(4 - step)]
            piece = block.at[pl.ds((step // 2) * (rows // 2), rows // 2)]
            post.send((w, "relay", step), piece, piece, sides[step])
            post.send((w, "cross", step), block, block, partner)

    def fifth(w):
        for step in (1, 3):
            post.arrived((w, "relay", step))
        block = hidden.at[core, w, chip(2)]
        post.send((w, "cross", 2), block, block, partner)

    stages = (first, second, third, fourth, fifth)
    for turn in range(waves + len(stages) - 1):
        for late in reversed(range(len(stages))):
            if 0 <= turn - late < waves:
                stages[late](turn - late)
    for w in range(waves):
        for piece in (0, 1, 3, 2):
            post.arrived((w, "cross", piece))
        pltpu.make_async_copy(made.at[w], hidden.at[core, w, y], puts.at[w]).wait()
    post.drain()


def call_blend(part, waves):
    cap, width = part.shape
    rows, units = cap // (8 * waves), width // 2
    hbm = pl.BlockSpec(memory_space=pl.ANY)
    hidden = pl.pallas_call(
        functools.partial(blend, waves),
        out_shape=jax.ShapeDtypeStruct((2, waves, SIDE, rows, units), BF16),
        in_specs=[hbm],
        out_specs=hbm,
        scratch_shapes=[
            pltpu.VMEM((waves, SIDE, rows, width), BF16),
            pltpu.VMEM((waves, SIDE, rows, width), BF16),
            pltpu.VMEM((waves, 2, rows, units), BF16),
            pltpu.VMEM((waves, 2, rows, units), BF16),
            pltpu.VMEM((waves, 2, rows, units), BF16),
            pltpu.VMEM((waves, 2, rows, units), BF16),
            pltpu.VMEM((waves, rows, units), BF16),
            pltpu.SemaphoreType.DMA((waves,)),
            pltpu.SemaphoreType.DMA((waves,)),
            pltpu.SemaphoreType.DMA((waves * 15,)),
            pltpu.SemaphoreType.DMA((waves * 15,)),
        ],
        compiler_params=pltpu.CompilerParams(
            collective_id=3, has_side_effects=True, vmem_limit_bytes=48 << 20
        ),
        name="blend",
    )(part.reshape(2, waves, SIDE, rows, width))
    return hidden.reshape(cap, units)


def slots_of(e, offs, base):
    low = jnp.clip(offs[e] - base[0], 0, CAP)
    return low, jnp.clip(offs[e + 1] - base[0], 0, CAP)


def mark(e, offs, base, pos, val, hot):
    rows = pos.shape[1]
    low, high = slots_of(e, offs, base)
    slot = lax.broadcasted_iota(I32, (ALIGN, rows), 0)

    def one(i, _):
        at = pl.multiple_of(low + i * ALIGN, ALIGN)
        value = 1.0 if val is None else val[pl.ds(e, 1), :]
        same = pos[pl.ds(e, 1), :] - at == slot
        hot[pl.ds(at, ALIGN), :] = jnp.where(same, value, 0.0).astype(BF16)
        return 0

    lax.fori_loop(0, lax.div(high - low, ALIGN), one, 0)


def blank(ref, low, high):
    def one(i, _):
        at = pl.multiple_of(low + i * ALIGN, ALIGN)
        ref[pl.ds(at, ALIGN), :] = jnp.zeros((ALIGN, ref.shape[1]), ref.dtype)
        return 0

    lax.fori_loop(0, lax.div(high - low, ALIGN), one, 0)


def spread(
    me, base, codes, tokens, weights, part, pos, val, offs, wbuf, sems, hot, xbuf, pbuf, osem
):
    experts = weights.shape[0]
    rows = tokens.shape[0]
    for e in range(experts):
        pltpu.make_async_copy(weights.at[e], wbuf.at[e], sems.at[e]).start()
    tri = (
        lax.broadcasted_iota(I32, (256, 256), 0) < lax.broadcasted_iota(I32, (256, 256), 1)
    ).astype(BF16)
    carry = jnp.zeros((experts, 1), F32)
    for c in range(rows // 256):
        span = slice(c * 256, (c + 1) * 256)
        code = codes[:, span]
        local = (code >> 4) - me[0] * experts
        gates = (code & 15).astype(F32)
        total = jnp.concatenate(
            [
                jnp.sum(jnp.where(local == e, gates, 0.0), axis=0, keepdims=True)
                for e in range(experts)
            ],
            axis=0,
        )
        chosen = (total > 0).astype(F32)
        before = jnp.dot(chosen.astype(BF16), tri, preferred_element_type=F32) + carry
        carry = carry + jnp.sum(chosen, axis=1, keepdims=True)
        val[:, span] = total
        pos[:, span] = jnp.where(total > 0, before, -1e6).astype(I32)
    row_of = lax.broadcasted_iota(I32, (experts, 1), 0)
    total = jnp.int32(0)
    starts = jnp.zeros((experts, 1), I32)
    for e in range(experts):
        count = jnp.sum(jnp.where(row_of == e, carry, 0.0)).astype(I32)
        offs[e] = total
        starts = jnp.where(row_of == e, total, starts)
        total += (count + ALIGN - 1) // ALIGN * ALIGN
    offs[experts] = total
    pos[...] += starts - base[0]
    end = jnp.clip(total - base[0], 0, CAP)
    tiles = lax.div(end + TILE - 1, TILE)

    def marks(e, _):
        mark(e, offs, base, pos, None, hot)
        return 0

    lax.fori_loop(0, experts, marks, 0)
    blank(hot, end, tiles * TILE)

    def gather(j, _):
        at = pl.multiple_of(j * TILE, TILE)
        xbuf[pl.ds(at, TILE), :] = jnp.dot(
            hot[pl.ds(at, TILE), :], tokens[...], preferred_element_type=F32
        ).astype(BF16)
        return 0

    lax.fori_loop(0, tiles, gather, 0)

    def put(j):
        at = pl.multiple_of(j * TILE, TILE)
        return pltpu.make_async_copy(
            pbuf.at[pl.ds(at, TILE)], part.at[pl.ds(at, TILE)], osem.at[j]
        )

    def start(j, _):
        put(j).start()
        return 0

    def group(e, sent):
        pltpu.make_async_copy(weights.at[e], wbuf.at[e], sems.at[e]).wait()
        low, high = slots_of(e, offs, base)

        def tile(i, _):
            at = pl.multiple_of(low + i * TILE, ALIGN)
            pbuf[pl.ds(at, TILE), :] = jnp.dot(
                xbuf[pl.ds(at, TILE), :], wbuf[e], preferred_element_type=F32
            ).astype(BF16)
            return 0

        lax.fori_loop(0, lax.div(high - low + TILE - 1, TILE), tile, 0)
        ready = lax.div(high, TILE)
        lax.fori_loop(sent, ready, start, 0)
        return ready

    sent = lax.fori_loop(0, experts, group, jnp.int32(0))
    blank(pbuf, end, CAP)
    lax.fori_loop(sent, CAP // TILE, start, 0)
    for j in range(CAP // TILE):
        put(j).wait()


def call_spread(me, base, codes, tokens, weights):
    experts, depth, width = weights.shape
    rows = tokens.shape[0]
    smem = pl.BlockSpec(memory_space=pltpu.SMEM)
    vmem = pl.BlockSpec(memory_space=pltpu.VMEM)
    hbm = pl.BlockSpec(memory_space=pl.ANY)
    return pl.pallas_call(
        spread,
        out_shape=(
            jax.ShapeDtypeStruct((CAP, width), BF16),
            jax.ShapeDtypeStruct((experts, rows), I32),
            jax.ShapeDtypeStruct((experts, rows), F32),
            jax.ShapeDtypeStruct((16,), I32),
        ),
        in_specs=[smem, smem, vmem, vmem, hbm],
        out_specs=(hbm, vmem, vmem, smem),
        scratch_shapes=[
            pltpu.VMEM(weights.shape, BF16),
            pltpu.SemaphoreType.DMA((experts,)),
            pltpu.VMEM((CAP, rows), BF16),
            pltpu.VMEM((CAP + TILE, depth), BF16),
            pltpu.VMEM((CAP + TILE, width), BF16),
            pltpu.SemaphoreType.DMA((CAP // TILE,)),
        ],
        compiler_params=pltpu.CompilerParams(vmem_limit_bytes=56 << 20),
        name="spread",
    )(me, base, codes, tokens, weights)


def collect(base, offs, pos, val, hidden, weights, out, wbuf, sems, hbuf, hsem, hot, rbuf, acc):
    experts = weights.shape[0]
    rows = pos.shape[1]
    for e in range(experts):
        pltpu.make_async_copy(weights.at[e], wbuf.at[e], sems.at[e]).start()
    for j in range(CAP // TILE):
        at = slice(j * TILE, (j + 1) * TILE)
        pltpu.make_async_copy(hidden.at[at], hbuf.at[at], hsem.at[j]).start()
    hbuf[CAP:, :] = jnp.zeros((TILE, hbuf.shape[1]), BF16)
    end = jnp.clip(offs[experts] - base[0], 0, CAP)
    tiles = lax.div(end + TILE - 1, TILE)

    def marks(e, _):
        mark(e, offs, base, pos, val, hot)
        return 0

    lax.fori_loop(0, experts, marks, 0)
    blank(hot, end, tiles * TILE)
    for j in range(CAP // TILE):
        at = slice(j * TILE, (j + 1) * TILE)
        pltpu.make_async_copy(hidden.at[at], hbuf.at[at], hsem.at[j]).wait()

    def group(e, _):
        pltpu.make_async_copy(weights.at[e], wbuf.at[e], sems.at[e]).wait()
        low, high = slots_of(e, offs, base)

        def tile(i, _):
            at = pl.multiple_of(low + i * TILE, ALIGN)
            rbuf[pl.ds(at, TILE), :] = lax.dot_general(
                hbuf[pl.ds(at, TILE), :],
                wbuf[e],
                (((1,), (1,)), ((), ())),
                preferred_element_type=F32,
            ).astype(BF16)
            return 0

        return lax.fori_loop(0, lax.div(high - low + TILE - 1, TILE), tile, 0)

    lax.fori_loop(0, experts, group, 0)
    blank(rbuf, end, tiles * TILE)
    acc[...] = jnp.zeros_like(acc)

    def combine(j, _):
        at = pl.multiple_of(j * TILE, TILE)
        turned = rbuf[pl.ds(at, TILE), :].astype(F32).T.astype(BF16)
        for c in range(rows // LANES):
            lane = slice(c * LANES, (c + 1) * LANES)
            acc[:, lane] += jnp.dot(
                turned, hot[pl.ds(at, TILE), lane], preferred_element_type=F32
            )
        return 0

    lax.fori_loop(0, tiles, combine, 0)

    def flip(c, _):
        lane = pl.multiple_of(c * 256, 256)
        out[pl.ds(lane, 256), :] = acc[:, pl.ds(lane, 256)].T.astype(out.dtype)
        return 0

    lax.fori_loop(0, rows // 256, flip, 0)


def call_collect(base, offs, pos, val, hidden, weights):
    experts, depth, width = weights.shape
    rows = pos.shape[1]
    smem = pl.BlockSpec(memory_space=pltpu.SMEM)
    vmem = pl.BlockSpec(memory_space=pltpu.VMEM)
    hbm = pl.BlockSpec(memory_space=pl.ANY)
    return pl.pallas_call(
        collect,
        out_shape=jax.ShapeDtypeStruct((rows, depth), BF16),
        in_specs=[smem, smem, vmem, vmem, hbm, hbm],
        out_specs=vmem,
        scratch_shapes=[
            pltpu.VMEM(weights.shape, BF16),
            pltpu.SemaphoreType.DMA((experts,)),
            pltpu.VMEM((CAP + TILE, width), BF16),
            pltpu.SemaphoreType.DMA((CAP // TILE,)),
            pltpu.VMEM((CAP, rows), BF16),
            pltpu.VMEM((CAP + TILE, depth), BF16),
            pltpu.VMEM((depth, rows), F32),
        ],
        compiler_params=pltpu.CompilerParams(vmem_limit_bytes=56 << 20),
        name="collect",
    )(base, offs, pos, val, hidden, weights)


def local(tokens, gate_up_weight, down_weight, placement, copy_ids, gate_codes):
    steps, rows, depth = tokens.shape
    experts = gate_up_weight.shape[0]
    top = copy_ids.shape[2]
    peers = lax.axis_size("ep")
    own = lax.axis_index("ep").astype(I32).reshape(1)
    ids = copy_ids.reshape(steps * rows, top).T
    same = ids[:, :, None] == jnp.arange(placement.shape[0], dtype=I32)
    expert = jnp.sum(jnp.where(same, placement, 0), axis=2)
    packed = expert * 16 + gate_codes.reshape(steps * rows, top).T
    codes, everyone = call_share(packed, tokens.reshape(steps * rows, depth))
    codes = codes.transpose(1, 0, 2).reshape(top, peers * steps * rows)
    everyone = everyone.reshape(peers * steps * rows, depth)
    tally = jnp.sum(
        (codes.reshape(-1) >> 4)[None, :] == jnp.arange(experts * peers, dtype=I32)[:, None],
        axis=1,
        dtype=I32,
    )
    most = jnp.max(jnp.sum(((tally + ALIGN - 1) // ALIGN * ALIGN).reshape(-1, experts), axis=1))

    def chunk(at):
        base = (at * CAP).reshape(1)
        part, pos, val, offs = call_spread(own, base, codes, everyone, gate_up_weight)
        hidden = call_blend(part, WAVES)
        return call_collect(base, offs, pos, val, hidden, down_weight)

    mixed = chunk(jnp.int32(0))
    _, mixed = lax.while_loop(
        lambda c: c[0] * CAP < most,
        lambda c: (c[0] + 1, (c[1].astype(F32) + chunk(c[0]).astype(F32)).astype(BF16)),
        (jnp.int32(1), mixed),
    )
    mixed = call_settle(mixed.reshape(SIDE, SIDE, steps * rows, depth))
    total = jnp.sum(gate_codes, axis=2).astype(F32)
    return (mixed.reshape(steps, rows, depth) / total[:, :, None]).astype(BF16)


def solution(mesh):
    in_specs = (
        P(None, "ep", "fsdp"),
        P("ep", "fsdp", None),
        P("ep", "fsdp", None),
        P(),
        P(None, "ep", None),
        P(None, "ep", None),
    )
    out_specs = P(None, "ep", "fsdp")
    return jax.shard_map(local, mesh=mesh, in_specs=in_specs, out_specs=out_specs, check_vma=False)
```

time: 301 us -> 147 us (0.49)
  waiting for transfers between devices: 175 us -> 0 us
  Pallas kernels: 77.5 us -> 135 us
  blocking collectives: 25.1 us -> 0 us
  between operations: 13.2 us -> 0.15 us
    reduce_scatter x2 -> x0, waiting for transfers between devices: 125 us -> none  [the longest x1 80.3 us: local(): lax.psum_scatter(mixed, 'ep', scatter_dimension=0, tiled=True).astype(F32)]
    pallas_call x0 -> x3, Pallas kernels: none -> 106 us  [the longest x1 56.5 us: call_blend(): pl.pallas_call(functools.partial(blend, waves), out_shape=jax.ShapeDtypeS...]
    all_gather x2 -> x0, waiting for transfers between devices: 48.5 us -> none  [the longest x1 27.9 us: chunk(): hidden = lax.all_gather(hidden, 'fsdp', axis=0, tiled=True)]
    pallas_call x1, Pallas kernels: 39.5 us -> 13.6 us  [call_spread(): pl.pallas_call(spread, out_shape=(jax.ShapeDtypeStruct((CAP, width), BF16...]
    all_gather x1 -> x0, blocking collectives: 25.1 us -> none  [local(): codes = lax.all_gather(packed, 'ep', axis=1, tiled=True)]
    pallas_call x1, Pallas kernels: 38 us -> 15.1 us  [call_collect(): pl.pallas_call(collect, out_shape=jax.ShapeDtypeStruct((rows, depth), BF1...]
  transfers between devices with their start and end apart: 4 -> 0, of which waited for: 4 -> 0; matrix products, arithmetic and copies ran while one was open for 2% -> 0% of each run, Pallas kernels for 0% -> 0%
where the time goes in v2:
time: 147 us; the launch traced here: 146 us
  Pallas kernels  135 us (92%)
  other arithmetic  5.31 us (4%)
  local copies, waits for them, and re-layouts  4.8 us (3%)
    pallas_call x1, Pallas kernels, call_blend(): pl.pallas_call(functools.partial(blend, waves), out_shape=jax.ShapeDtypeS...  56.5 us
    pallas_call x1, Pallas kernels, call_settle(): pl.pallas_call(settle, out_shape=jax.ShapeDtypeStruct((rows, depth), F32)...  25.8 us
    pallas_call x1, Pallas kernels, call_share(): pl.pallas_call(share, out_shape=(jax.ShapeDtypeStruct((peers,) + codes.sh...  23.7 us
    pallas_call x1, Pallas kernels, call_collect(): pl.pallas_call(collect, out_shape=jax.ShapeDtypeStruct((rows, depth), BF1...  15.1 us
    pallas_call x1, Pallas kernels, call_spread(): pl.pallas_call(spread, out_shape=(jax.ShapeDtypeStruct((CAP, width), BF16...  13.6 us
    unnamed x12, local copies, waits for them, and re-layouts  3.21 us

profile of v2, /device:TPU:8, one launch (start us, length us, event | category | flops | bytes accessed | tf_op | source)
XLA Modules:
  0.0 145.8 jit_solution(4260234612260729761)
XLA Ops:
  0.0 0.7 copy.15
  0.7 0.1 reshape.56
  0.8 0.7 copy.14
  1.5 0.1 reshape.55
  1.6 1.0 select_reduce_fusion
  2.6 0.6 bitcast_add_fusion.codes
  3.2 23.7 %share.1 = (s32[16,8,192]{2,1,0:T(8,128)}, bf16[16,192,256]{2,1,0:T(8,128)(2,1)S(1)}) custom-call(s32[8,192]{1,0:T(8,128)} %bitcast_add_fusion.codes, bf16[192,256]{1,0:T(8,128)(2,1)} %bitcast.34), custom_call_target="tpu_custom_call" | custom-call | tf_op jit(solution)/shard_map/share/pallas_call | solution.py:148
  26.9 0.0 copy-start.5
  26.9 1.1 copy.16
  28.0 0.1 reshape.58.codes
  28.1 13.6 %spread.2 = (bf16[2304,1536]{1,0:T(8,128)(2,1)}, s32[8,3072]{1,0:T(8,128)}, f32[8,3072]{1,0:T(8,128)}, s32[16]{0:T(128)}) custom-call(s32[1]{0:T(128)} %bitcast.3.me, s32[1]{0:T(128)} %constant.32.clone.1.base, s32[8,3072]{1,0:T(8,128)S(1)} %reshape.58.codes, bf16[3072,256]{1,0:T(8,128)(2,1)S(1)} %bitcast.29, bf16[8,256,1536]{2,1,0:T(8,128)(2,1)} %weights.2), custom_call_target="tpu_custom_call" | custom-call | tf_op jit(solution)/shard_map/spread/pallas_call | solution.py:506
  41.7 0.0 copy-start.2
  41.8 56.5 %blend.2 = bf16[2,6,4,48,768]{4,3,2,1,0:T(8,128)(2,1)S(1)} custom-call(bf16[2,6,4,48,1536]{4,3,2,1,0:T(8,128)(2,1)} %bitcast.31), custom_call_target="tpu_custom_call" | custom-call | tf_op jit(solution)/shard_map/blend/pallas_call | solution.py:355
  98.3 1.7 %copy-done.1 = bf16[2,6,4,48,768]{4,3,2,1,0:T(8,128)(2,1)} copy-done((bf16[2,6,4,48,768]{4,3,2,1,0:T(8,128)(2,1)}, bf16[2,6,4,48,768]{4,3,2,1,0:T(8,128)(2,1)S(1)}, u32[]{:S(2)}) %copy-start.1) | copy-done | bytes 3538968
  100.0 15.1 %collect.2 = bf16[3072,256]{1,0:T(8,128)(2,1)} custom-call(s32[1]{0:T(128)} %constant.32.clone.1.base, s32[16]{0:T(128)} %get-tuple-element.60.offs, s32[8,3072]{1,0:T(8,128)} %get-tuple-element.61.pos, f32[8,3072]{1,0:T(8,128)} %get-tuple-element.62.val, bf16[2304,768]{1,0:T(8,128)(2,1)} %bitcast.26, bf16[8,256,768]{2,1,0:T(8,128)(2,1)S(1)} %copy-done.2), custom_call_target="tpu_custom_call" | custom-call | tf_op jit(solution)/shard_map/collect/pallas_call | solution.py:597
  115.2 0.1 shift_right_arithmetic.15
  115.3 1.3 convert_reduce_fusion
  116.7 0.1 sub.18
  116.7 0.1 fusion.2
  116.9 0.6 reduce_max.9
  117.5 0.7 while.10
  118.2 0.0 copy-start.7
  118.2 25.8 %settle.1 = f32[192,256]{1,0:T(8,128)} custom-call(bf16[4,4,192,256]{3,2,1,0:T(8,128)(2,1)} %bitcast.28), custom_call_target="tpu_custom_call" | custom-call | tf_op jit(solution)/shard_map/settle/pallas_call | solution.py:243
  144.1 1.7 %divide_convert_fusion = bf16[4,48,256]{2,1,0:T(8,128)(2,1)} fusion(f32[4,48,256]{2,1,0:T(8,128)} %bitcast.32, f32[4,48]{1,0:T(4,128)S(1)} %convert_element_type.23), kind=kLoop, calls=%fused_computation.5 | loop fusion | flops 98304 | bytes 295680 | tf_op jit(solution)/shard_map/convert_element_type | solution.py:650
  (11 shorter events, 0.1 us)
Async XLA Ops:
  26.9 14.8 %copy-start.5 = (bf16[16,192,256]{2,1,0:T(8,128)(2,1)}, bf16[16,192,256]{2,1,0:T(8,128)(2,1)S(1)}, u32[]{:S(2)}) copy-start(bf16[16,192,256]{2,1,0:T(8,128)(2,1)S(1)} %get-tuple-element.59) | copy-start | bytes 4718596
  41.7 58.3 %copy-start.2 = (bf16[8,256,768]{2,1,0:T(8,128)(2,1)S(1)}, bf16[8,256,768]{2,1,0:T(8,128)(2,1)}, u32[]{:S(2)}) copy-start(bf16[8,256,768]{2,1,0:T(8,128)(2,1)} %weights.3) | copy-start | bytes 9437188
  98.3 1.8 %copy-start.1 = (bf16[2,6,4,48,768]{4,3,2,1,0:T(8,128)(2,1)}, bf16[2,6,4,48,768]{4,3,2,1,0:T(8,128)(2,1)S(1)}, u32[]{:S(2)}) copy-start(bf16[2,6,4,48,768]{4,3,2,1,0:T(8,128)(2,1)S(1)} %blend.2) | copy-start | bytes 10616836
  100.0 15.1 %copy-start.6 = (s32[16,8,192]{2,1,0:T(8,128)S(1)}, s32[16,8,192]{2,1,0:T(8,128)}, u32[]{:S(2)}) copy-start(s32[16,8,192]{2,1,0:T(8,128)} %get-tuple-element.58) | copy-start | bytes 294916
  118.2 25.8 %copy-start.7 = (s32[4,48,8]{1,2,0:T(8,128)S(1)}, s32[4,48,8]{1,2,0:T(8,128)}, u32[]{:S(2)}) copy-start(s32[4,48,8]{1,2,0:T(8,128)} %param.13) | copy-start | bytes 18436

commit v3 on v2

v3 whole, which is shorter than its diff:
```python
import functools

import jax
import jax.numpy as jnp
from jax import lax
from jax.experimental import pallas as pl
from jax.experimental.pallas import tpu as pltpu
from jax.sharding import PartitionSpec as P

I32, F32, BF16 = jnp.int32, jnp.float32, jnp.bfloat16
TILE = 64
LANES = 512
CHOICES = (7, 8, 9, 10)
MESH = pl.DeviceIdType.MESH
SIDE = 4
LOW, HIGH = 0, 1


class Post:
    def __init__(self, sends, recvs):
        self.sends, self.recvs, self.made = sends, recvs, {}

    def send(self, key, src, dst, target):
        number = self.made.setdefault(key, len(self.made))
        copy = pltpu.make_async_remote_copy(
            src_ref=src,
            dst_ref=dst,
            send_sem=self.sends.at[number],
            recv_sem=self.recvs.at[number],
            device_id=target,
            device_id_type=MESH,
        )
        copy.start()
        self.made[key] = number
        setattr(self, "copy_%d" % number, copy)

    def arrived(self, key):
        getattr(self, "copy_%d" % self.made[key]).wait_recv()

    def drain(self):
        for number in self.made.values():
            getattr(self, "copy_%d" % number).wait_send()


def greet(targets):
    barrier = pltpu.get_barrier_semaphore()
    for target in targets:
        pl.semaphore_signal(barrier, inc=1, device_id=target, device_id_type=MESH)
    pl.semaphore_wait(barrier, len(targets))


def torus():
    me = lax.axis_index("ep")
    z, x = lax.div(me, SIDE), lax.rem(me, SIDE)

    def at(dz, dx):
        return lax.rem(z + dz, SIDE) * SIDE + lax.rem(x + dx, SIDE)

    return me, z, x, at


def share(codes, tokens, codes_all, tokens_all, keep, csend, crecv, sends, recvs):
    me, z, x, at = torus()
    greet([{"ep": lax.rem(me + d, SIDE * SIDE)} for d in range(1, SIDE * SIDE)])
    rows, depth = tokens.shape
    half = depth // 2
    near = []
    for d in range(1, SIDE * SIDE):
        copy = pltpu.make_async_remote_copy(
            src_ref=codes,
            dst_ref=codes_all.at[me],
            send_sem=csend.at[d],
            recv_sem=crecv.at[d],
            device_id={"ep": lax.rem(me + d, SIDE * SIDE)},
            device_id_type=MESH,
        )
        copy.start()
        near.append(copy)
    post = Post(sends, recvs)
    mine = pltpu.make_async_copy(tokens, tokens_all.at[me], keep.at[0])
    mine.start()
    mine_codes = pltpu.make_async_copy(codes, codes_all.at[me], keep.at[1])
    mine_codes.start()

    def place(side, first, second):
        return at(second, first) if side == 0 else at(first, second)

    def block(side, first, second, part=None):
        span = slice(None) if part is None else pl.ds(part * (rows // 2), rows // 2)
        return tokens_all.at[place(side, first, second), span, pl.ds(side * half, half)]

    def target(side, axis, step):
        first, second = (step, 0) if axis == 1 else (0, step)
        return {"ep": place(side, first, second)}

    for axis in (1, 2):
        for side in (0, 1):
            own = tokens.at[:, pl.ds(side * half, half)]
            for step in (1, 3):
                post.send((side, axis, 0, step), own, block(side, 0, 0), target(side, axis, step))

    def onward(side, first):
        src = block(side, first, 0)
        for step in (1, 3):
            post.send((side, 2, first, step), src, src, target(side, 2, step))

    for step in (1, 3):
        for side in (0, 1):
            post.arrived((side, 1, 0, step))
            part = LOW if step == 1 else HIGH
            src = block(side, 4 - step, 0, part)
            post.send((side, 1, "far", step), src, src, target(side, 1, step))
            onward(side, 4 - step)

    def relay(side, first):
        for step in (1, 3):
            post.arrived((side, 2, first, step))
            part = LOW if step == 1 else HIGH
            src = block(side, first, 4 - step, part)
            post.send((side, 2, first, "far", step), src, src, target(side, 2, step))

    for side in (0, 1):
        relay(side, 0)
    for side in (0, 1):
        for step in (1, 3):
            post.arrived((side, 1, "far", step))
        onward(side, 2)
    for first in (3, 1, 2):
        for side in (0, 1):
            relay(side, first)
    for first in (0, 3, 1, 2):
        for side in (0, 1):
            for step in (1, 3):
                post.arrived((side, 2, first, "far", step))
    for copy in near:
        copy.wait()
    post.drain()
    mine.wait()
    mine_codes.wait()


def call_share(codes, tokens):
    peers = SIDE * SIDE
    vmem = pl.BlockSpec(memory_space=pltpu.VMEM)
    hbm = pl.BlockSpec(memory_space=pl.ANY)
    return pl.pallas_call(
        share,
        out_shape=(
            jax.ShapeDtypeStruct((peers,) + codes.shape, codes.dtype),
            jax.ShapeDtypeStruct((peers,) + tokens.shape, tokens.dtype),
        ),
        in_specs=[vmem, vmem],
        out_specs=(hbm, hbm),
        scratch_shapes=[
            pltpu.SemaphoreType.DMA((2,)),
            pltpu.SemaphoreType.DMA((peers,)),
            pltpu.SemaphoreType.DMA((peers,)),
            pltpu.SemaphoreType.DMA((40,)),
            pltpu.SemaphoreType.DMA((40,)),
        ],
        compiler_params=pltpu.CompilerParams(collective_id=1, has_side_effects=True),
        name="share",
    )(codes, tokens)


def settle(parts, out, big, mid, small, tiny, sends, recvs):
    me, z, x, at = torus()
    greet([{"ep": at(0, 1)}, {"ep": at(0, 3)}, {"ep": at(1, 0)}, {"ep": at(3, 0)}])
    rows, depth = parts.shape[2:]
    half, lot = depth // 2, rows // 2
    post = Post(sends, recvs)
    axis_one = (x, z)
    axis_two = (z, x)

    def wide(side, step, part):
        to = lax.rem(axis_one[side] + step, SIDE)
        spot = (slice(None), to) if side == 0 else (to, slice(None))
        return parts.at[spot + (pl.ds(part * lot, lot), pl.ds(side * half, half))]

    def target(side, stage, step):
        along_x = (side == 0) == (stage == 1)
        return {"ep": at(0, step) if along_x else at(step, 0)}

    def add(a, b):
        return a[...].astype(F32) + b[...].astype(F32)

    def ring(side, stage, source, slots, fill):
        go = functools.partial(target, side, stage)
        yield
        post.send((side, stage, 0), source(2, LOW), slots.at[0], go(1))
        post.send((side, stage, 1), source(2, HIGH), slots.at[1], go(3))
        yield
        post.send((side, stage, 3), source(1, HIGH), slots.at[3], go(1))
        post.send((side, stage, 2), source(3, LOW), slots.at[2], go(3))
        yield
        post.arrived((side, stage, 0))
        fill[0] = add(source(1, LOW), slots.at[0]).astype(BF16)
        post.send((side, stage, 4), fill.at[0], slots.at[4], go(1))
        post.arrived((side, stage, 1))
        fill[1] = add(source(3, HIGH), slots.at[1]).astype(BF16)
        post.send((side, stage, 5), fill.at[1], slots.at[5], go(3))
        yield
        for slot in (2, 3, 4, 5):
            post.arrived((side, stage, slot))
        yield

    def run(stage, sources, slots, fill):
        rings = [ring(side, stage, sources[side], slots.at[side], fill.at[side]) for side in (0, 1)]
        for _ in range(5):
            for one in rings:
                next(one)

    run(1, [functools.partial(wide, side) for side in (0, 1)], big, mid.at[0])
    sums = mid.at[1]
    for side in (0, 1):
        for part in (LOW, HIGH):
            sums[side, part] = (
                wide(side, 0, part)[...].astype(F32)
                + big[side, 2 + part].astype(F32)
                + big[side, 4 + part].astype(F32)
            ).astype(BF16)

    def narrow(side, step, part):
        return sums.at[side, part, lax.rem(axis_two[side] + step, SIDE)]

    run(2, [functools.partial(narrow, side) for side in (0, 1)], small, tiny)
    for side in (0, 1):
        for part in (LOW, HIGH):
            out[pl.ds(part * lot, lot), pl.ds(side * half, half)] = (
                narrow(side, 0, part)[...].astype(F32)
                + small[side, 2 + part].astype(F32)
                + small[side, 4 + part].astype(F32)
            )
    post.drain()


def call_settle(parts):
    rows, depth = parts.shape[2:]
    lot, half = rows // 2, depth // 2
    vmem = pl.BlockSpec(memory_space=pltpu.VMEM)
    return pl.pallas_call(
        settle,
        out_shape=jax.ShapeDtypeStruct((rows, depth), F32),
        in_specs=[vmem],
        out_specs=vmem,
        scratch_shapes=[
            pltpu.VMEM((2, 6, SIDE, lot, half), BF16),
            pltpu.VMEM((2, 2, 2, SIDE, lot, half), BF16),
            pltpu.VMEM((2, 6, lot, half), BF16),
            pltpu.VMEM((2, 2, lot, half), BF16),
            pltpu.SemaphoreType.DMA((24,)),
            pltpu.SemaphoreType.DMA((24,)),
        ],
        compiler_params=pltpu.CompilerParams(collective_id=2, has_side_effects=True),
        name="settle",
    )(parts)


WAVE = 256
DEPTH = 8
ORDER = (5, 4, 3, 2, 1, 0, 6)
KINDS = (("swap", 0), ("cross", 4), ("cross", 2)) + tuple(
    (name, step)
    for name in ("far", "direct", "summed", "round", "relay", "cross")
    for step in (1, 3)
)


def route(me, base, codes, pos, val, table):
    experts = pos.shape[0]
    peers, _, rows = codes.shape
    code = jnp.concatenate([codes[p] for p in range(peers)], axis=1)
    tri = (
        lax.broadcasted_iota(I32, (256, 256), 0) < lax.broadcasted_iota(I32, (256, 256), 1)
    ).astype(BF16)
    carry = jnp.zeros((experts, 1), F32)
    for c in range(peers * rows // 256):
        span = slice(c * 256, (c + 1) * 256)
        local = (code[:, span] >> 4) - me[0] * experts
        gates = (code[:, span] & 15).astype(F32)
        total = jnp.concatenate(
            [
                jnp.sum(jnp.where(local == e, gates, 0.0), axis=0, keepdims=True)
                for e in range(experts)
            ],
            axis=0,
        )
        chosen = (total > 0).astype(F32)
        before = jnp.dot(chosen.astype(BF16), tri, preferred_element_type=F32) + carry
        carry = carry + jnp.sum(chosen, axis=1, keepdims=True)
        val[:, span] = total
        pos[:, span] = jnp.where(total > 0, before, -1e6).astype(I32)
    sizes = (carry.astype(I32) + TILE - 1) // TILE * TILE
    row_of = lax.broadcasted_iota(I32, (experts, 1), 0)
    starts = jnp.zeros((experts, 1), I32)
    for e in range(experts - 1):
        starts = starts + jnp.where(row_of > e, sizes[e : e + 1, :], 0)
    pos[...] += starts - base[0]
    slot = lax.broadcasted_iota(I32, (experts, 128), 1) * TILE + base[0]
    past = jnp.where(starts + sizes <= slot, 1, 0)
    table[...] = jnp.minimum(jnp.sum(past, axis=0, keepdims=True), experts - 1)


def call_route(me, base, codes, experts):
    peers, _, rows = codes.shape
    smem = pl.BlockSpec(memory_space=pltpu.SMEM)
    vmem = pl.BlockSpec(memory_space=pltpu.VMEM)
    return pl.pallas_call(
        route,
        out_shape=(
            jax.ShapeDtypeStruct((experts, peers * rows), I32),
            jax.ShapeDtypeStruct((experts, peers * rows), F32),
            jax.ShapeDtypeStruct((1, 128), I32),
        ),
        in_specs=[smem, smem, vmem],
        out_specs=(vmem, vmem, vmem),
        name="route",
    )(me, base, codes)


def core(
    waves,
    table,
    pos,
    val,
    tokens,
    gate_up,
    down,
    out,
    wide,
    narrow,
    wsems,
    hot,
    scale,
    picked,
    parts,
    other,
    far,
    direct,
    summed,
    fill,
    hidden,
    turned,
    acc,
    sends,
    recvs,
):
    me = lax.axis_index("fsdp")
    y, core_at = lax.div(me, 2), lax.rem(me, 2)
    experts, units = down.shape[0], down.shape[2]
    rows = WAVE // 8
    side = WAVE // 2
    tiles = WAVE // TILE
    partner = {"fsdp": y * 2 + 1 - core_at}
    sides = {step: {"fsdp": lax.rem(y + step, SIDE) * 2 + core_at} for step in (1, 3)}
    loads = []
    for e in range(experts):
        loads.append(pltpu.make_async_copy(gate_up.at[e], wide.at[e], wsems.at[e]))
    for e in range(experts):
        loads.append(pltpu.make_async_copy(down.at[e], narrow.at[e], wsems.at[experts + e]))
    for load in loads:
        load.start()
    greet([partner, sides[1], sides[3]])
    columns = (pl.ds(0, units), pl.ds(units, units))

    def half(which):
        return pl.ds(pl.multiple_of(which * side, side), side)

    def block(step):
        at = core_at * side + lax.rem(y + step, SIDE) * rows
        return pl.ds(pl.multiple_of(at, rows), rows)

    def mine(w, step, piece):
        return parts.at[w, block(step), columns[piece]]

    def route_of(kind, w):
        name, step = kind
        piece = LOW if (step == 1) == (name != "direct") else HIGH
        if name == "swap":
            return parts.at[w, half(1 - core_at)], other.at[w], partner
        if name == "far":
            return mine(w, 2, piece), far.at[w, piece], sides[step]
        if name == "direct":
            return mine(w, step, piece), direct.at[w, piece], sides[step]
        if name == "summed":
            return fill.at[w, piece], summed.at[w, piece], sides[step]
        if name == "round":
            own = hidden.at[w, block(0)]
            return own, own, sides[step]
        if name == "cross":
            whole = hidden.at[w, block(4 - step)]
            return whole, whole, partner
        at = core_at * side + lax.rem(y + 4 - step, SIDE) * rows + (step // 2) * (rows // 2)
        part = hidden.at[w, pl.ds(pl.multiple_of(at, rows // 2), rows // 2)]
        return part, part, sides[step]

    def copy(name, step, w):
        src, dst, to = route_of((name, step), w)
        k = KINDS.index((name, step))
        return pltpu.make_async_remote_copy(
            src_ref=src,
            dst_ref=dst,
            send_sem=sends.at[w, k],
            recv_sem=recvs.at[w, k],
            device_id=to,
            device_id_type=MESH,
        )

    slot = lax.broadcasted_iota(I32, (TILE, pos.shape[1]), 0)

    def produce(w):
        spot = lax.rem(w, DEPTH)

        def mark(j, _):
            e = table[w * tiles + j]
            at = pl.multiple_of(j * TILE, TILE)
            same = pos[pl.ds(e, 1), :] - (w * WAVE + at) == slot
            hot[spot, pl.ds(at, TILE), :] = jnp.where(same, 1.0, 0.0).astype(BF16)
            scale[spot, pl.ds(at, TILE), :] = jnp.sum(
                jnp.where(same, val[pl.ds(e, 1), :], 0.0), axis=1, keepdims=True
            )
            return 0

        lax.fori_loop(0, tiles, mark, 0)
        picked[...] = jnp.dot(hot[spot], tokens[...], preferred_element_type=F32).astype(BF16)

        @pl.when(w == 0)
        def _():
            for load in loads[:experts]:
                load.wait()

        def tile(which, j, _):
            j = which * (tiles // 2) + j
            e = table[w * tiles + j]
            at = pl.ds(pl.multiple_of(j * TILE, TILE), TILE)
            parts[w, at, :] = jnp.dot(
                picked[at, :], wide[e], preferred_element_type=F32
            ).astype(BF16)
            return 0

        lax.fori_loop(0, tiles // 2, functools.partial(tile, 1 - core_at), 0)
        copy("swap", 0, w).start()
        lax.fori_loop(0, tiles // 2, functools.partial(tile, core_at), 0)

    def fold(w, step):
        at = pl.ds(pl.multiple_of(lax.rem(y + step, SIDE) * rows, rows), rows)
        parts[w, block(step), :] = parts[w, block(step), :] + other[w, at, :]

    def first(w):
        copy("swap", 0, w).wait_recv()
        fold(w, 2)
        copy("far", 1, w).start()
        copy("far", 3, w).start()
        fold(w, 1)
        copy("direct", 1, w).start()
        fold(w, 3)
        copy("direct", 3, w).start()
        fold(w, 0)

    def second(w):
        for piece, step in ((LOW, 1), (HIGH, 3)):
            copy("far", step, w).wait_recv()
            fill[w, piece] = mine(w, step, piece)[...] + far[w, piece]
            copy("summed", step, w).start()

    def third(w):
        both = []
        for piece, step in ((LOW, 1), (HIGH, 3)):
            copy("direct", 4 - step, w).wait_recv()
            copy("summed", step, w).wait_recv()
            both.append(
                mine(w, 0, piece)[...].astype(F32)
                + direct[w, piece].astype(F32)
                + summed[w, piece].astype(F32)
            )
        gate, up = both
        hidden[w, block(0), :] = (gate / (1 + jnp.exp(-gate)) * up).astype(BF16)
        copy("round", 1, w).start()
        copy("round", 3, w).start()
        copy("cross", 4, w).start()

    def fourth(w):
        for step in (1, 3):
            copy("round", step, w).wait_recv()
            copy("relay", step, w).start()
            copy("cross", step, w).start()

    def fifth(w):
        for step in (1, 3):
            copy("relay", step, w).wait_recv()
        copy("cross", 2, w).start()

    def consume(w):
        spot = lax.rem(w, DEPTH)

        @pl.when(w == 0)
        def _():
            for load in loads[experts:]:
                load.wait()

        for step in (4, 1, 3, 2):
            copy("cross", step, w).wait_recv()

        def tile(j, _):
            e = table[w * tiles + j]
            at = pl.ds(pl.multiple_of(j * TILE, TILE), TILE)
            result = lax.dot_general(
                hidden[w, at, :], narrow[e], (((1,), (1,)), ((), ())), preferred_element_type=F32
            )
            turned[at, :] = result * scale[spot, at, :]
            return 0

        lax.fori_loop(0, tiles, tile, 0)
        flat = turned[...].T.astype(BF16)
        for c in range(pos.shape[1] // LANES):
            lane = pl.ds(c * LANES, LANES)
            acc[:, lane] += jnp.dot(flat, hot[spot, :, lane], preferred_element_type=F32)

    acc[...] = jnp.zeros_like(acc)
    stages = (produce, first, second, third, fourth, fifth, consume)

    def turn(t, _):
        for late in ORDER:
            w = t - late

            @pl.when((w >= 0) & (w < waves))
            def _(late=late, w=w):
                stages[late](w)

        return 0

    lax.fori_loop(0, waves + len(stages) - 1, turn, 0)

    def flip(c, _):
        lane = pl.multiple_of(c * 256, 256)
        out[pl.ds(lane, 256), :] = acc[:, pl.ds(lane, 256)].T.astype(out.dtype)
        return 0

    lax.fori_loop(0, out.shape[0] // 256, flip, 0)

    def drain(w, _):
        for name, step in KINDS:
            copy(name, step, w).wait_send()
        return 0

    lax.fori_loop(0, waves, drain, 0)


def call_core(waves, table, pos, val, tokens, gate_up, down):
    experts, depth, width = gate_up.shape
    rows, units = WAVE // 8, width // 2
    total = tokens.shape[0]
    smem = pl.BlockSpec(memory_space=pltpu.SMEM)
    vmem = pl.BlockSpec(memory_space=pltpu.VMEM)
    hbm = pl.BlockSpec(memory_space=pl.ANY)
    piece = pltpu.VMEM((waves, 2, rows, units), BF16)
    return pl.pallas_call(
        functools.partial(core, waves),
        out_shape=jax.ShapeDtypeStruct((total, depth), BF16),
        in_specs=[smem, vmem, vmem, vmem, hbm, hbm],
        out_specs=vmem,
        scratch_shapes=[
            pltpu.VMEM(gate_up.shape, BF16),
            pltpu.VMEM(down.shape, BF16),
            pltpu.SemaphoreType.DMA((2 * experts,)),
            pltpu.VMEM((DEPTH, WAVE, total), BF16),
            pltpu.VMEM((DEPTH, WAVE, 1), F32),
            pltpu.VMEM((WAVE, depth), BF16),
            pltpu.VMEM((waves, WAVE, width), BF16),
            pltpu.VMEM((waves, WAVE // 2, width), BF16),
            piece,
            piece,
            piece,
            piece,
            pltpu.VMEM((waves, WAVE, units), BF16),
            pltpu.VMEM((WAVE, depth), F32),
            pltpu.VMEM((depth, total), F32),
            pltpu.SemaphoreType.DMA((waves, len(KINDS))),
            pltpu.SemaphoreType.DMA((waves, len(KINDS))),
        ],
        compiler_params=pltpu.CompilerParams(
            collective_id=waves, has_side_effects=True, vmem_limit_bytes=62 << 20
        ),
        name="core%d" % waves,
    )(table, pos, val, tokens, gate_up, down)


def local(tokens, gate_up_weight, down_weight, placement, copy_ids, gate_codes):
    steps, rows, depth = tokens.shape
    experts = gate_up_weight.shape[0]
    top = copy_ids.shape[2]
    peers = lax.axis_size("ep")
    own = lax.axis_index("ep").astype(I32).reshape(1)
    ids = copy_ids.reshape(steps * rows, top).T
    same = ids[:, :, None] == jnp.arange(placement.shape[0], dtype=I32)
    expert = jnp.sum(jnp.where(same, placement, 0), axis=2)
    packed = expert * 16 + gate_codes.reshape(steps * rows, top).T
    codes, everyone = call_share(packed, tokens.reshape(steps * rows, depth))
    everyone = everyone.reshape(peers * steps * rows, depth)
    tally = jnp.sum(
        (codes >> 4)[None] == jnp.arange(experts * peers, dtype=I32)[:, None, None, None],
        axis=(1, 2, 3),
        dtype=I32,
    )
    most = jnp.max(jnp.sum(((tally + TILE - 1) // TILE * TILE).reshape(-1, experts), axis=1))

    def chunk(base, waves):
        pos, val, table = call_route(own, base.reshape(1), codes, experts)
        return call_core(waves, table.reshape(-1), pos, val, everyone, gate_up_weight, down_weight)

    pos, val, table = call_route(own, jnp.zeros((1,), I32), codes, experts)
    branches = [functools.partial(call_core, waves) for waves in CHOICES]
    pick = jnp.int32(0)
    for waves in CHOICES[:-1]:
        pick += (most > waves * WAVE).astype(I32)
    mixed = lax.switch(
        pick, branches, table.reshape(-1), pos, val, everyone, gate_up_weight, down_weight
    )
    span = CHOICES[-1] * WAVE
    _, mixed = lax.while_loop(
        lambda c: c[0] * span < most,
        lambda c: (
            c[0] + 1,
            (c[1].astype(F32) + chunk(c[0] * span, CHOICES[-1]).astype(F32)).astype(BF16),
        ),
        (jnp.int32(1), mixed),
    )
    mixed = call_settle(mixed.reshape(SIDE, SIDE, steps * rows, depth))
    total = jnp.sum(gate_codes, axis=2).astype(F32)
    return (mixed.reshape(steps, rows, depth) / total[:, :, None]).astype(BF16)


def solution(mesh):
    in_specs = (
        P(None, "ep", "fsdp"),
        P("ep", "fsdp", None),
        P("ep", "fsdp", None),
        P(),
        P(None, "ep", None),
        P(None, "ep", None),
    )
    out_specs = P(None, "ep", "fsdp")
    return jax.shard_map(local, mesh=mesh, in_specs=in_specs, out_specs=out_specs, check_vma=False)
```

time: 147 us -> 130 us (0.88)
  Pallas kernels: 135 us -> 116 us
  other arithmetic: 5.31 us -> 8.67 us
  local copies, waits for them, and re-layouts: 4.8 us -> 1.7 us
  between operations: 0.15 us -> 2.12 us
    pallas_call x3 -> x2, Pallas kernels: 85.3 us -> 70.3 us  [the longest x1 69.8 us: call_core(): pl.pallas_call(functools.partial(core, waves), out_shape=jax.ShapeDtypeSt...]
    pallas_call x1, Pallas kernels: 25.8 us -> 21.8 us  [call_settle(): pl.pallas_call(settle, out_shape=jax.ShapeDtypeStruct((rows, depth), F32)...]
    reduce_sum x2, other arithmetic: 1.43 us -> 4.68 us  [the longest x1 4.56 us: local(): jnp.sum((codes >> 4)[None] == jnp.arange(experts * peers, dtype=I32)[:, N...]
    unnamed x12 -> x4, local copies, waits for them, and re-layouts: 3.21 us -> 1.45 us
where the time goes in v3:
time: 130 us; the launch traced here: 129 us
  Pallas kernels  116 us (89%)
  other arithmetic  8.67 us (7%)
  between operations  2.12 us (2%)
  local copies, waits for them, and re-layouts  1.7 us (1%)
    pallas_call x1, Pallas kernels, call_core(): pl.pallas_call(functools.partial(core, waves), out_shape=jax.ShapeDtypeSt...  69.8 us
    pallas_call x1, Pallas kernels, call_share(): pl.pallas_call(share, out_shape=(jax.ShapeDtypeStruct((peers,) + codes.sh...  23.8 us
    pallas_call x1, Pallas kernels, call_settle(): pl.pallas_call(settle, out_shape=jax.ShapeDtypeStruct((rows, depth), F32)...  21.8 us
    reduce_sum x1, other arithmetic, local(): jnp.sum((codes >> 4)[None] == jnp.arange(experts * peers, dtype=I32)[:, N...  4.56 us

profile of v3, /device:TPU:8, one launch (start us, length us, event | category | flops | bytes accessed | tf_op | source)
XLA Modules:
  0.0 129.4 jit_solution(17920112757930002336)
XLA Ops:
  0.0 0.7 copy.11
  0.7 0.1 reshape.39
  0.8 1.0 select_reduce_fusion
  1.8 0.7 copy.12
  2.5 0.1 reshape.40
  2.6 0.6 bitcast_add_fusion.codes
  3.2 23.8 %share.1 = (s32[16,8,192]{2,1,0:T(8,128)S(1)}, bf16[16,192,256]{2,1,0:T(8,128)(2,1)S(1)}) custom-call(s32[8,192]{1,0:T(8,128)} %bitcast_add_fusion.codes, bf16[192,256]{1,0:T(8,128)(2,1)} %bitcast.26), custom_call_target="tpu_custom_call" | custom-call | tf_op jit(solution)/shard_map/share/pallas_call | solution.py:146
  26.9 0.5 route.2
  27.5 4.6 %convert_reduce_fusion = s32[128]{0:T(128)S(1)} fusion(s32[16,8,192]{2,1,0:T(8,128)S(1)} %broadcast_shift-right-arithmetic_fusion), kind=kLoop, calls=%fused_computation.1 | loop fusion | flops 9437056 | bytes 98816 | tf_op jit(solution)/shard_map/reduce_sum | solution.py:600
  32.0 0.1 sub.18
  32.1 0.1 fusion.2
  32.2 0.7 reduce_max.9
  35.0 70.2 %conditional.1 = (bf16[3072,256]{1,0:T(8,128)(2,1)}) conditional(s32[]{:T(128)} %clamp.3, (s32[128]{0:T(128)S(1)}, s32[8,3072]{1,0:T(8,128)S(1)}, f32[8,3072]{1,0:T(8,128)S(1)}, bf16[3072,256]{1,0:T(8,128)(2,1)S(1)}, bf16[8,256,1536]{2,1,0:T(8,128)(2,1)}, /*index=5*/bf16[8,256,768]{2,1,0:T(8,128)(2,1)}) %tuple.43, ...), branch_computations={%region_4.5_spmd, %region_5.6_spmd, %region_6.7_spmd, %region_7.8_... | conditional | bytes 8 | solution.py:616
  35.0 69.8 %core9.1 = bf16[3072,256]{1,0:T(8,128)(2,1)} custom-call(s32[128]{0:T(128)S(1)} %get-tuple-element.102.table, s32[8,3072]{1,0:T(8,128)S(1)} %get-tuple-element.103.pos, f32[8,3072]{1,0:T(8,128)S(1)} %get-tuple-element.104.val, bf16[3072,256]{1,0:T(8,128)(2,1)S(1)} %get-tuple-element.105.tokens, bf16[8,256,1536]{2,1,0:T(8,128)(2,1)} %get-tuple-element.106.gate_up, ...), custom_call_target="tpu_custom_call" | custom-call | tf_op jit(solution)/shard_map/cond/branch_2_fun/core9/pallas_call | solution.py:557
  105.2 0.7 while.10
  105.9 0.0 copy-start
  105.9 21.8 %settle.1 = f32[192,256]{1,0:T(8,128)} custom-call(bf16[4,4,192,256]{3,2,1,0:T(8,128)(2,1)} %bitcast.24), custom_call_target="tpu_custom_call" | custom-call | tf_op jit(solution)/shard_map/settle/pallas_call | solution.py:241
  127.7 0.0 copy-done
  127.8 1.7 %divide_convert_fusion = bf16[4,48,256]{2,1,0:T(8,128)(2,1)} fusion(f32[4,48,256]{2,1,0:T(8,128)} %bitcast.25, f32[4,48]{1,0:T(4,128)S(1)} %convert_element_type.35), kind=kLoop, calls=%fused_computation.5 | loop fusion | flops 98304 | bytes 295680 | tf_op jit(solution)/shard_map/convert_element_type | solution.py:630
  (4 shorter events, 0.0 us)
Async XLA Ops:
  105.9 21.8 %copy-start = (s32[4,48,8]{1,2,0:T(8,128)S(1)}, s32[4,48,8]{1,2,0:T(8,128)}, u32[]{:S(2)}) copy-start(s32[4,48,8]{1,2,0:T(8,128)} %param.17) | copy-start | bytes 18436

commit v4 on v3

--- a/solution.py
+++ b/solution.py
@@ -59,28 +59,27 @@
     return me, z, x, at
 
 
-def share(codes, tokens, codes_all, tokens_all, keep, csend, crecv, sends, recvs):
+def share(raw, placement, tokens, codes_all, tokens_all, codes, keep, sends, recvs):
     me, z, x, at = torus()
-    greet([{"ep": lax.rem(me + d, SIDE * SIDE)} for d in range(1, SIDE * SIDE)])
+    barrier = pltpu.get_barrier_semaphore()
+    peers = [(0, step) for step in (1, 2, 3)] + [(step, 0) for step in (1, 2, 3)]
+    for dz, dx in peers:
+        pl.semaphore_signal(barrier, inc=1, device_id={"ep": at(dz, dx)}, device_id_type=MESH)
+    copies = raw[...] >> 4
+
+    def look(i, found):
+        return jnp.where(copies == i, placement[i], found)
+
+    found = lax.fori_loop(0, placement.shape[0], look, jnp.zeros_like(copies), unroll=8)
+    codes[...] = found * 16 + (raw[...] & 15)
+    pl.semaphore_wait(barrier, len(peers))
     rows, depth = tokens.shape
     half = depth // 2
-    near = []
-    for d in range(1, SIDE * SIDE):
-        copy = pltpu.make_async_remote_copy(
-            src_ref=codes,
-            dst_ref=codes_all.at[me],
-            send_sem=csend.at[d],
-            recv_sem=crecv.at[d],
-            device_id={"ep": lax.rem(me + d, SIDE * SIDE)},
-            device_id_type=MESH,
-        )
-        copy.start()
-        near.append(copy)
     post = Post(sends, recvs)
-    mine = pltpu.make_async_copy(tokens, tokens_all.at[me], keep.at[0])
-    mine.start()
-    mine_codes = pltpu.make_async_copy(codes, codes_all.at[me], keep.at[1])
+    mine_codes = pltpu.make_async_copy(codes, codes_all.at[z, x], keep.at[1])
     mine_codes.start()
+    for step in (1, 3, 2):
+        post.send(("codes", 1, step), codes, codes_all.at[z, x], {"ep": at(0, step)})
 
     def place(side, first, second):
         return at(second, first) if side == 0 else at(first, second)
@@ -93,24 +92,18 @@
         first, second = (step, 0) if axis == 1 else (0, step)
         return {"ep": place(side, first, second)}
 
-    for axis in (1, 2):
+    for axis, steps in ((1, (2, 1, 3)), (2, (1, 3))):
         for side in (0, 1):
             own = tokens.at[:, pl.ds(side * half, half)]
-            for step in (1, 3):
+            for step in steps:
                 post.send((side, axis, 0, step), own, block(side, 0, 0), target(side, axis, step))
-
-    def onward(side, first):
+    mine = pltpu.make_async_copy(tokens, tokens_all.at[me], keep.at[0])
+    mine.start()
+
+    def onward(side, first, steps):
         src = block(side, first, 0)
-        for step in (1, 3):
+        for step in steps:
             post.send((side, 2, first, step), src, src, target(side, 2, step))
-
-    for step in (1, 3):
-        for side in (0, 1):
-            post.arrived((side, 1, 0, step))
-            part = LOW if step == 1 else HIGH
-            src = block(side, 4 - step, 0, part)
-            post.send((side, 1, "far", step), src, src, target(side, 1, step))
-            onward(side, 4 - step)
 
     def relay(side, first):
         for step in (1, 3):
@@ -119,53 +112,60 @@
             src = block(side, first, 4 - step, part)
             post.send((side, 2, first, "far", step), src, src, target(side, 2, step))
 
+    for step in (1, 3, 2):
+        post.arrived(("codes", 1, step))
+    mine_codes.wait()
+    for step in (1, 3, 2):
+        post.send(("codes", 2, step), codes_all.at[z], codes_all.at[z], {"ep": at(step, 0)})
+    for step in (1, 3):
+        for side in (0, 1):
+            post.arrived((side, 1, 0, step))
+            onward(side, 4 - step, (1, 3))
     for side in (0, 1):
-        relay(side, 0)
-    for side in (0, 1):
-        for step in (1, 3):
-            post.arrived((side, 1, "far", step))
-        onward(side, 2)
-    for first in (3, 1, 2):
+        post.arrived((side, 1, 0, 2))
+        onward(side, 2, (2, 1, 3))
+    for first in (0, 3, 1):
         for side in (0, 1):
             relay(side, first)
-    for first in (0, 3, 1, 2):
+    for first in (0, 3, 1):
         for side in (0, 1):
             for step in (1, 3):
                 post.arrived((side, 2, first, "far", step))
-    for copy in near:
-        copy.wait()
+    for side in (0, 1):
+        for step in (1, 3, 2):
+            post.arrived((side, 2, 2, step))
+    for step in (1, 3, 2):
+        post.arrived(("codes", 2, step))
     post.drain()
     mine.wait()
-    mine_codes.wait()
-
-
-def call_share(codes, tokens):
-    peers = SIDE * SIDE
+
+
+def call_share(raw, placement, tokens):
     vmem = pl.BlockSpec(memory_space=pltpu.VMEM)
+    smem = pl.BlockSpec(memory_space=pltpu.SMEM)
     hbm = pl.BlockSpec(memory_space=pl.ANY)
     return pl.pallas_call(
         share,
         out_shape=(
-            jax.ShapeDtypeStruct((peers,) + codes.shape, codes.dtype),
-            jax.ShapeDtypeStruct((peers,) + tokens.shape, tokens.dtype),
+            jax.ShapeDtypeStruct((SIDE, SIDE) + raw.shape, raw.dtype),
+            jax.ShapeDtypeStruct((SIDE * SIDE,) + tokens.shape, tokens.dtype),
         ),
-        in_specs=[vmem, vmem],
+        in_specs=[vmem, smem, vmem],
         out_specs=(hbm, hbm),
         scratch_shapes=[
+            pltpu.VMEM(raw.shape, raw.dtype),
             pltpu.SemaphoreType.DMA((2,)),
-            pltpu.SemaphoreType.DMA((peers,)),
-            pltpu.SemaphoreType.DMA((peers,)),
-            pltpu.SemaphoreType.DMA((40,)),
-            pltpu.SemaphoreType.DMA((40,)),
+            pltpu.SemaphoreType.DMA((42,)),
+            pltpu.SemaphoreType.DMA((42,)),
         ],
         compiler_params=pltpu.CompilerParams(collective_id=1, has_side_effects=True),
         name="share",
-    )(codes, tokens)
-
-
-def settle(parts, out, big, mid, small, tiny, sends, recvs):
+    )(raw, placement, tokens)
+
+
+def settle(parts, out, big, fills, sums, small, sends, recvs):
     me, z, x, at = torus()
-    greet([{"ep": at(0, 1)}, {"ep": at(0, 3)}, {"ep": at(1, 0)}, {"ep": at(3, 0)}])
+    greet([{"ep": at(0, step)} for step in (1, 2, 3)] + [{"ep": at(step, 0)} for step in (1, 2, 3)])
     rows, depth = parts.shape[2:]
     half, lot = depth // 2, rows // 2
     post = Post(sends, recvs)
@@ -181,56 +181,38 @@
         along_x = (side == 0) == (stage == 1)
         return {"ep": at(0, step) if along_x else at(step, 0)}
 
-    def add(a, b):
-        return a[...].astype(F32) + b[...].astype(F32)
-
-    def ring(side, stage, source, slots, fill):
-        go = functools.partial(target, side, stage)
-        yield
-        post.send((side, stage, 0), source(2, LOW), slots.at[0], go(1))
-        post.send((side, stage, 1), source(2, HIGH), slots.at[1], go(3))
-        yield
-        post.send((side, stage, 3), source(1, HIGH), slots.at[3], go(1))
-        post.send((side, stage, 2), source(3, LOW), slots.at[2], go(3))
-        yield
-        post.arrived((side, stage, 0))
-        fill[0] = add(source(1, LOW), slots.at[0]).astype(BF16)
-        post.send((side, stage, 4), fill.at[0], slots.at[4], go(1))
-        post.arrived((side, stage, 1))
-        fill[1] = add(source(3, HIGH), slots.at[1]).astype(BF16)
-        post.send((side, stage, 5), fill.at[1], slots.at[5], go(3))
-        yield
-        for slot in (2, 3, 4, 5):
-            post.arrived((side, stage, slot))
-        yield
-
-    def run(stage, sources, slots, fill):
-        rings = [ring(side, stage, sources[side], slots.at[side], fill.at[side]) for side in (0, 1)]
-        for _ in range(5):
-            for one in rings:
-                next(one)
-
-    run(1, [functools.partial(wide, side) for side in (0, 1)], big, mid.at[0])
-    sums = mid.at[1]
     for side in (0, 1):
-        for part in (LOW, HIGH):
-            sums[side, part] = (
+        post.send((side, 0), wide(side, 2, LOW), big.at[side, 0], target(side, 1, 1))
+        post.send((side, 1), wide(side, 2, HIGH), big.at[side, 1], target(side, 1, 3))
+    for side in (0, 1):
+        post.send((side, 3), wide(side, 1, HIGH), big.at[side, 3], target(side, 1, 1))
+        post.send((side, 2), wide(side, 3, LOW), big.at[side, 2], target(side, 1, 3))
+    for side in (0, 1):
+        for part, step in ((LOW, 1), (HIGH, 3)):
+            post.arrived((side, part))
+            fills[side, part] = wide(side, step, part)[...] + big[side, part]
+            post.send((side, 4 + part), fills.at[side, part], big.at[side, 4 + part], target(side, 1, step))
+    for side in (0, 1):
+        for part in (HIGH, LOW):
+            post.arrived((side, 2 + part))
+            post.arrived((side, 4 + part))
+            sums[side, :, pl.ds(part * lot, lot), :] = (
                 wide(side, 0, part)[...].astype(F32)
                 + big[side, 2 + part].astype(F32)
                 + big[side, 4 + part].astype(F32)
             ).astype(BF16)
-
-    def narrow(side, step, part):
-        return sums.at[side, part, lax.rem(axis_two[side] + step, SIDE)]
-
-    run(2, [functools.partial(narrow, side) for side in (0, 1)], small, tiny)
+        for step in (2, 1, 3):
+            to = lax.rem(axis_two[side] + step, SIDE)
+            post.send((side, "two", step), sums.at[side, to], small.at[side, step - 1], target(side, 2, step))
     for side in (0, 1):
-        for part in (LOW, HIGH):
-            out[pl.ds(part * lot, lot), pl.ds(side * half, half)] = (
-                narrow(side, 0, part)[...].astype(F32)
-                + small[side, 2 + part].astype(F32)
-                + small[side, 4 + part].astype(F32)
-            )
+        for step in (1, 3, 2):
+            post.arrived((side, "two", step))
+        out[:, pl.ds(side * half, half)] = (
+            sums[side, axis_two[side]].astype(F32)
+            + small[side, 0].astype(F32)
+            + small[side, 1].astype(F32)
+            + small[side, 2].astype(F32)
+        )
     post.drain()
 
 
@@ -245,11 +227,11 @@
         out_specs=vmem,
         scratch_shapes=[
             pltpu.VMEM((2, 6, SIDE, lot, half), BF16),
-            pltpu.VMEM((2, 2, 2, SIDE, lot, half), BF16),
-            pltpu.VMEM((2, 6, lot, half), BF16),
-            pltpu.VMEM((2, 2, lot, half), BF16),
-            pltpu.SemaphoreType.DMA((24,)),
-            pltpu.SemaphoreType.DMA((24,)),
+            pltpu.VMEM((2, 2, SIDE, lot, half), BF16),
+            pltpu.VMEM((2, SIDE, rows, half), BF16),
+            pltpu.VMEM((2, 3, rows, half), BF16),
+            pltpu.SemaphoreType.DMA((18,)),
+            pltpu.SemaphoreType.DMA((18,)),
         ],
         compiler_params=pltpu.CompilerParams(collective_id=2, has_side_effects=True),
         name="settle",
@@ -266,7 +248,7 @@
 )
 
 
-def route(me, base, codes, pos, val, table):
+def route(me, base, codes, pos, val, table, most):
     experts = pos.shape[0]
     peers, _, rows = codes.shape
     code = jnp.concatenate([codes[p] for p in range(peers)], axis=1)
@@ -299,6 +281,21 @@
     slot = lax.broadcasted_iota(I32, (experts, 128), 1) * TILE + base[0]
     past = jnp.where(starts + sizes <= slot, 1, 0)
     table[...] = jnp.minimum(jnp.sum(past, axis=0, keepdims=True), experts - 1)
+    named = jnp.zeros((peers, experts), F32)
+    owner_of = lax.broadcasted_iota(I32, (peers, code.shape[1]), 0)
+    local_of = lax.broadcasted_iota(I32, (experts, code.shape[1]), 0)
+    for k in range(code.shape[0]):
+        expert = code[k : k + 1, :] >> 4
+        owner = lax.div(expert, experts)
+        named = named + lax.dot_general(
+            (owner == owner_of).astype(F32).astype(BF16),
+            (expert - owner * experts == local_of).astype(F32).astype(BF16),
+            (((1,), (1,)), ((), ())),
+            preferred_element_type=F32,
+        )
+    padded = (named.astype(I32) + TILE - 1) // TILE * TILE
+    load = jnp.max(jnp.sum(padded, axis=1, keepdims=True), axis=0, keepdims=True)
+    most[...] = jnp.broadcast_to(load, most.shape)
 
 
 def call_route(me, base, codes, experts):
@@ -311,9 +308,10 @@
             jax.ShapeDtypeStruct((experts, peers * rows), I32),
             jax.ShapeDtypeStruct((experts, peers * rows), F32),
             jax.ShapeDtypeStruct((1, 128), I32),
+            jax.ShapeDtypeStruct((1, 128), I32),
         ),
         in_specs=[smem, smem, vmem],
-        out_specs=(vmem, vmem, vmem),
+        out_specs=(vmem, vmem, vmem, vmem),
         name="route",
     )(me, base, codes)
 
@@ -591,24 +589,17 @@
     top = copy_ids.shape[2]
     peers = lax.axis_size("ep")
     own = lax.axis_index("ep").astype(I32).reshape(1)
-    ids = copy_ids.reshape(steps * rows, top).T
-    same = ids[:, :, None] == jnp.arange(placement.shape[0], dtype=I32)
-    expert = jnp.sum(jnp.where(same, placement, 0), axis=2)
-    packed = expert * 16 + gate_codes.reshape(steps * rows, top).T
-    codes, everyone = call_share(packed, tokens.reshape(steps * rows, depth))
+    raw = (copy_ids * 16 + gate_codes).reshape(steps * rows, top).T
+    codes, everyone = call_share(raw, placement, tokens.reshape(steps * rows, depth))
+    codes = codes.reshape(peers, top, steps * rows)
     everyone = everyone.reshape(peers * steps * rows, depth)
-    tally = jnp.sum(
-        (codes >> 4)[None] == jnp.arange(experts * peers, dtype=I32)[:, None, None, None],
-        axis=(1, 2, 3),
-        dtype=I32,
-    )
-    most = jnp.max(jnp.sum(((tally + TILE - 1) // TILE * TILE).reshape(-1, experts), axis=1))
 
     def chunk(base, waves):
-        pos, val, table = call_route(own, base.reshape(1), codes, experts)
+        pos, val, table, _ = call_route(own, base.reshape(1), codes, experts)
         return call_core(waves, table.reshape(-1), pos, val, everyone, gate_up_weight, down_weight)
 
-    pos, val, table = call_route(own, jnp.zeros((1,), I32), codes, experts)
+    pos, val, table, most = call_route(own, jnp.zeros((1,), I32), codes, experts)
+    most = most[0, 0]
     branches = [functools.partial(call_core, waves) for waves in CHOICES]
     pick = jnp.int32(0)
     for waves in CHOICES[:-1]:

time: 130 us -> 115 us (0.88)
  Pallas kernels: 116 us -> 109 us
  other arithmetic: 8.67 us -> 2.43 us
  between operations: 2.12 us -> 0.17 us
    reduce_sum x3 -> x0, other arithmetic: 5.64 us -> none  [the longest x1 4.56 us: local(): jnp.sum((codes >> 4)[None] == jnp.arange(experts * peers, dtype=I32)[:, N...]
    pallas_call x1, Pallas kernels: 21.8 us -> 17.8 us  [call_settle(): pl.pallas_call(settle, out_shape=jax.ShapeDtypeStruct((rows, depth), F32)...]
    pallas_call x1, Pallas kernels: 23.8 us -> 20.7 us  [call_share(): pl.pallas_call(share, out_shape=(jax.ShapeDtypeStruct((SIDE, SIDE) + raw....]
where the time goes in v4:
time: 115 us; the launch traced here: 114 us
  Pallas kernels  109 us (95%)
  other arithmetic  2.43 us (2%)
    pallas_call x1, Pallas kernels, call_core(): pl.pallas_call(functools.partial(core, waves), out_shape=jax.ShapeDtypeSt...  69.7 us
    pallas_call x1, Pallas kernels, call_share(): pl.pallas_call(share, out_shape=(jax.ShapeDtypeStruct((SIDE, SIDE) + raw....  20.7 us
    pallas_call x1, Pallas kernels, call_settle(): pl.pallas_call(settle, out_shape=jax.ShapeDtypeStruct((rows, depth), F32)...  17.8 us

profile of v4, /device:TPU:8, one launch (start us, length us, event | category | flops | bytes accessed | tf_op | source)
XLA Modules:
  0.0 114.0 jit_solution(13620144032299009724)
XLA Ops:
  0.0 0.8 fusion
  0.8 0.7 reshape.34
  1.5 20.7 %share.1 = (s32[4,4,8,192]{3,2,1,0:T(8,128)S(1)}, bf16[16,192,256]{2,1,0:T(8,128)(2,1)S(1)}) custom-call(s32[8,192]{1,0:T(8,128)} %bitcast.28, s32[160]{0:T(256)} %placement.1, bf16[192,256]{1,0:T(8,128)(2,1)} %bitcast.27), custom_call_target="tpu_custom_call" | custom-call | tf_op jit(solution)/shard_map/share/pallas_call | solution.py:147
  22.2 1.2 %route.2 = (s32[8,3072]{1,0:T(8,128)S(1)}, f32[8,3072]{1,0:T(8,128)S(1)}, s32[1,128]{1,0:T(1,128)S(1)}, s32[1,128]{1,0:T(1,128)S(1)}) custom-call(s32[1]{0:T(128)} %bitcast.2.me, s32[1]{0:T(128)} %constant.9.clone.1.base, s32[16,8,192]{2,1,0:T(8,128)S(1)} %bitcast.24), custom_call_target="tpu_custom_call" | custom-call | tf_op jit(solution)/shard_map/route/pallas_call | solution.py:305
  23.4 0.0 copy-start
  23.5 0.4 copy-done
  23.9 70.1 %conditional.1 = (bf16[3072,256]{1,0:T(8,128)(2,1)}) conditional(s32[]{:T(128)} %clamp.3, (s32[128]{0:T(128)S(1)}, s32[8,3072]{1,0:T(8,128)S(1)}, f32[8,3072]{1,0:T(8,128)S(1)}, bf16[3072,256]{1,0:T(8,128)(2,1)S(1)}, bf16[8,256,1536]{2,1,0:T(8,128)(2,1)}, /*index=5*/bf16[8,256,768]{2,1,0:T(8,128)(2,1)}) %tuple.45, ...), branch_computations={%region_0.0_spmd, %region_1.0_spmd, %region_2.0_spmd, %region_3.0_... | conditional | bytes 8 | solution.py:607
  23.9 69.7 %core9.1 = bf16[3072,256]{1,0:T(8,128)(2,1)} custom-call(s32[128]{0:T(128)S(1)} %get-tuple-element.102.table, s32[8,3072]{1,0:T(8,128)S(1)} %get-tuple-element.103.pos, f32[8,3072]{1,0:T(8,128)S(1)} %get-tuple-element.104.val, bf16[3072,256]{1,0:T(8,128)(2,1)S(1)} %get-tuple-element.105.tokens, bf16[8,256,1536]{2,1,0:T(8,128)(2,1)} %get-tuple-element.106.gate_up, ...), custom_call_target="tpu_custom_call" | custom-call | tf_op jit(solution)/shard_map/cond/branch_2_fun/core9/pallas_call | solution.py:555
  94.0 0.6 while.10
  94.6 17.8 %settle.1 = f32[192,256]{1,0:T(8,128)} custom-call(bf16[4,4,192,256]{3,2,1,0:T(8,128)(2,1)} %bitcast.23), custom_call_target="tpu_custom_call" | custom-call | tf_op jit(solution)/shard_map/settle/pallas_call | solution.py:223
  112.4 1.7 %divide_convert_fusion = bf16[4,48,256]{2,1,0:T(8,128)(2,1)} fusion(f32[4,48,256]{2,1,0:T(8,128)} %bitcast.26, f32[4,48]{1,0:T(4,128)S(1)} %convert_element_type.31), kind=kLoop, calls=%fused_computation.1 | loop fusion | flops 98304 | bytes 295680 | tf_op jit(solution)/shard_map/convert_element_type | solution.py:621
  (2 shorter events, 0.0 us)
Async XLA Ops:
  23.4 0.5 copy-start

commit v5 on v4

--- a/solution.py
+++ b/solution.py
@@ -8,8 +8,9 @@
 from jax.sharding import PartitionSpec as P
 
 I32, F32, BF16 = jnp.int32, jnp.float32, jnp.bfloat16
-TILE = 64
+TILE = 32
 LANES = 512
+TABLE = 512
 CHOICES = (7, 8, 9, 10)
 MESH = pl.DeviceIdType.MESH
 SIDE = 4
@@ -59,25 +60,90 @@
     return me, z, x, at
 
 
-def share(raw, placement, tokens, codes_all, tokens_all, codes, keep, sends, recvs):
+def routing(me, pieces, pos, val, table, most):
+    experts = pos.shape[0]
+    peers = SIDE * SIDE
+    code = jnp.concatenate(pieces, axis=1)
+    tri = (
+        lax.broadcasted_iota(I32, (256, 256), 0) < lax.broadcasted_iota(I32, (256, 256), 1)
+    ).astype(F32).astype(BF16)
+    carry = jnp.zeros((experts, 1), F32)
+    for c in range(code.shape[1] // 256):
+        span = slice(c * 256, (c + 1) * 256)
+        local = (code[:, span] >> 4) - me * experts
+        gates = (code[:, span] & 15).astype(F32)
+        total = jnp.concatenate(
+            [
+                jnp.sum(jnp.where(local == e, gates, 0.0), axis=0, keepdims=True)
+                for e in range(experts)
+            ],
+            axis=0,
+        )
+        chosen = (total > 0).astype(F32)
+        before = jnp.dot(chosen.astype(BF16), tri, preferred_element_type=F32) + carry
+        carry = carry + jnp.sum(chosen, axis=1, keepdims=True)
+        val[:, span] = total
+        pos[:, span] = jnp.where(total > 0, before, -1e6).astype(I32)
+    sizes = (carry.astype(I32) + TILE - 1) // TILE * TILE
+    row_of = lax.broadcasted_iota(I32, (experts, 1), 0)
+    starts = jnp.zeros((experts, 1), I32)
+    for e in range(experts - 1):
+        starts = starts + jnp.where(row_of > e, sizes[e : e + 1, :], 0)
+    pos[...] += starts
+    slot = lax.broadcasted_iota(I32, (experts, table.shape[1]), 1) * TILE
+    past = jnp.where(starts + sizes <= slot, 1, 0)
+    table[...] = jnp.minimum(jnp.sum(past, axis=0, keepdims=True), experts - 1)
+    named = jnp.zeros((peers, experts), F32)
+    owner_of = lax.broadcasted_iota(I32, (peers, code.shape[1]), 0)
+    local_of = lax.broadcasted_iota(I32, (experts, code.shape[1]), 0)
+    for k in range(code.shape[0]):
+        expert = code[k : k + 1, :] >> 4
+        owner = lax.div(expert, experts)
+        named = named + lax.dot_general(
+            (owner == owner_of).astype(F32).astype(BF16),
+            (expert - owner * experts == local_of).astype(F32).astype(BF16),
+            (((1,), (1,)), ((), ())),
+            preferred_element_type=F32,
+        )
+    padded = (named.astype(I32) + TILE - 1) // TILE * TILE
+    load = jnp.max(jnp.sum(padded, axis=1, keepdims=True), axis=0, keepdims=True)
+    most[...] = jnp.broadcast_to(load, most.shape)
+
+
+def share(
+    ids,
+    gates,
+    placement,
+    tokens,
+    tokens_all,
+    pos,
+    val,
+    table,
+    most,
+    totals,
+    codes_all,
+    keep,
+    sends,
+    recvs,
+):
     me, z, x, at = torus()
     barrier = pltpu.get_barrier_semaphore()
     peers = [(0, step) for step in (1, 2, 3)] + [(step, 0) for step in (1, 2, 3)]
     for dz, dx in peers:
         pl.semaphore_signal(barrier, inc=1, device_id={"ep": at(dz, dx)}, device_id_type=MESH)
-    copies = raw[...] >> 4
+    copies = ids[...]
 
     def look(i, found):
         return jnp.where(copies == i, placement[i], found)
 
     found = lax.fori_loop(0, placement.shape[0], look, jnp.zeros_like(copies), unroll=8)
-    codes[...] = found * 16 + (raw[...] & 15)
+    codes_all[z, x] = found * 16 + gates[...]
+    totals[...] = jnp.sum(gates[...].astype(F32), axis=1)
+    codes = codes_all.at[z, x]
     pl.semaphore_wait(barrier, len(peers))
     rows, depth = tokens.shape
     half = depth // 2
     post = Post(sends, recvs)
-    mine_codes = pltpu.make_async_copy(codes, codes_all.at[z, x], keep.at[1])
-    mine_codes.start()
     for step in (1, 3, 2):
         post.send(("codes", 1, step), codes, codes_all.at[z, x], {"ep": at(0, step)})
 
@@ -114,7 +180,6 @@
 
     for step in (1, 3, 2):
         post.arrived(("codes", 1, step))
-    mine_codes.wait()
     for step in (1, 3, 2):
         post.send(("codes", 2, step), codes_all.at[z], codes_all.at[z], {"ep": at(step, 0)})
     for step in (1, 3):
@@ -127,6 +192,15 @@
     for first in (0, 3, 1):
         for side in (0, 1):
             relay(side, first)
+    for step in (1, 3, 2):
+        post.arrived(("codes", 2, step))
+    pieces = [
+        codes_all[far, near, step]
+        for far in range(SIDE)
+        for near in range(SIDE)
+        for step in range(ids.shape[0])
+    ]
+    routing(me, pieces, pos, val, table, most)
     for first in (0, 3, 1):
         for side in (0, 1):
             for step in (1, 3):
@@ -134,33 +208,37 @@
     for side in (0, 1):
         for step in (1, 3, 2):
             post.arrived((side, 2, 2, step))
-    for step in (1, 3, 2):
-        post.arrived(("codes", 2, step))
     post.drain()
     mine.wait()
 
 
-def call_share(raw, placement, tokens):
+def call_share(ids, gates, placement, tokens, experts):
     vmem = pl.BlockSpec(memory_space=pltpu.VMEM)
     smem = pl.BlockSpec(memory_space=pltpu.SMEM)
     hbm = pl.BlockSpec(memory_space=pl.ANY)
+    peers = SIDE * SIDE
+    total = peers * tokens.shape[0]
     return pl.pallas_call(
         share,
         out_shape=(
-            jax.ShapeDtypeStruct((SIDE, SIDE) + raw.shape, raw.dtype),
-            jax.ShapeDtypeStruct((SIDE * SIDE,) + tokens.shape, tokens.dtype),
+            jax.ShapeDtypeStruct((peers,) + tokens.shape, tokens.dtype),
+            jax.ShapeDtypeStruct((experts, total), I32),
+            jax.ShapeDtypeStruct((experts, total), F32),
+            jax.ShapeDtypeStruct((1, TABLE), I32),
+            jax.ShapeDtypeStruct((1, 128), I32),
+            jax.ShapeDtypeStruct((ids.shape[0], ids.shape[2]), F32),
         ),
-        in_specs=[vmem, smem, vmem],
-        out_specs=(hbm, hbm),
+        in_specs=[vmem, vmem, smem, vmem],
+        out_specs=(hbm, vmem, vmem, vmem, vmem, vmem),
         scratch_shapes=[
-            pltpu.VMEM(raw.shape, raw.dtype),
-            pltpu.SemaphoreType.DMA((2,)),
+            pltpu.VMEM((SIDE, SIDE) + ids.shape, ids.dtype),
+            pltpu.SemaphoreType.DMA((1,)),
             pltpu.SemaphoreType.DMA((42,)),
             pltpu.SemaphoreType.DMA((42,)),
         ],
         compiler_params=pltpu.CompilerParams(collective_id=1, has_side_effects=True),
         name="share",
-    )(raw, placement, tokens)
+    )(ids, gates, placement, tokens)
 
 
 def settle(parts, out, big, fills, sums, small, sends, recvs):
@@ -239,81 +317,13 @@
 
 
 WAVE = 256
-DEPTH = 8
+DEPTH = 7
 ORDER = (5, 4, 3, 2, 1, 0, 6)
 KINDS = (("swap", 0), ("cross", 4), ("cross", 2)) + tuple(
     (name, step)
     for name in ("far", "direct", "summed", "round", "relay", "cross")
     for step in (1, 3)
 )
-
-
-def route(me, base, codes, pos, val, table, most):
-    experts = pos.shape[0]
-    peers, _, rows = codes.shape
-    code = jnp.concatenate([codes[p] for p in range(peers)], axis=1)
-    tri = (
-        lax.broadcasted_iota(I32, (256, 256), 0) < lax.broadcasted_iota(I32, (256, 256), 1)
-    ).astype(BF16)
-    carry = jnp.zeros((experts, 1), F32)
-    for c in range(peers * rows // 256):
-        span = slice(c * 256, (c + 1) * 256)
-        local = (code[:, span] >> 4) - me[0] * experts
-        gates = (code[:, span] & 15).astype(F32)
-        total = jnp.concatenate(
-            [
-                jnp.sum(jnp.where(local == e, gates, 0.0), axis=0, keepdims=True)
-                for e in range(experts)
-            ],
-            axis=0,
-        )
-        chosen = (total > 0).astype(F32)
-        before = jnp.dot(chosen.astype(BF16), tri, preferred_element_type=F32) + carry
-        carry = carry + jnp.sum(chosen, axis=1, keepdims=True)
-        val[:, span] = total
-        pos[:, span] = jnp.where(total > 0, before, -1e6).astype(I32)
-    sizes = (carry.astype(I32) + TILE - 1) // TILE * TILE
-    row_of = lax.broadcasted_iota(I32, (experts, 1), 0)
-    starts = jnp.zeros((experts, 1), I32)
-    for e in range(experts - 1):
-        starts = starts + jnp.where(row_of > e, sizes[e : e + 1, :], 0)
-    pos[...] += starts - base[0]
-    slot = lax.broadcasted_iota(I32, (experts, 128), 1) * TILE + base[0]
-    past = jnp.where(starts + sizes <= slot, 1, 0)
-    table[...] = jnp.minimum(jnp.sum(past, axis=0, keepdims=True), experts - 1)
-    named = jnp.zeros((peers, experts), F32)
-    owner_of = lax.broadcasted_iota(I32, (peers, code.shape[1]), 0)
-    local_of = lax.broadcasted_iota(I32, (experts, code.shape[1]), 0)
-    for k in range(code.shape[0]):
-        expert = code[k : k + 1, :] >> 4
-        owner = lax.div(expert, experts)
-        named = named + lax.dot_general(
-            (owner == owner_of).astype(F32).astype(BF16),
-            (expert - owner * experts == local_of).astype(F32).astype(BF16),
-            (((1,), (1,)), ((), ())),
-            preferred_element_type=F32,
-        )
-    padded = (named.astype(I32) + TILE - 1) // TILE * TILE
-    load = jnp.max(jnp.sum(padded, axis=1, keepdims=True), axis=0, keepdims=True)
-    most[...] = jnp.broadcast_to(load, most.shape)
-
-
-def call_route(me, base, codes, experts):
-    peers, _, rows = codes.shape
-    smem = pl.BlockSpec(memory_space=pltpu.SMEM)
-    vmem = pl.BlockSpec(memory_space=pltpu.VMEM)
-    return pl.pallas_call(
-        route,
-        out_shape=(
-            jax.ShapeDtypeStruct((experts, peers * rows), I32),
-            jax.ShapeDtypeStruct((experts, peers * rows), F32),
-            jax.ShapeDtypeStruct((1, 128), I32),
-            jax.ShapeDtypeStruct((1, 128), I32),
-        ),
-        in_specs=[smem, smem, vmem],
-        out_specs=(vmem, vmem, vmem, vmem),
-        name="route",
-    )(me, base, codes)
 
 
 def core(
@@ -327,9 +337,10 @@
     out,
     wide,
     narrow,
+    flipped,
     wsems,
     hot,
-    scale,
+    plain,
     picked,
     parts,
     other,
@@ -413,14 +424,12 @@
             e = table[w * tiles + j]
             at = pl.multiple_of(j * TILE, TILE)
             same = pos[pl.ds(e, 1), :] - (w * WAVE + at) == slot
-            hot[spot, pl.ds(at, TILE), :] = jnp.where(same, 1.0, 0.0).astype(BF16)
-            scale[spot, pl.ds(at, TILE), :] = jnp.sum(
-                jnp.where(same, val[pl.ds(e, 1), :], 0.0), axis=1, keepdims=True
-            )
+            plain[pl.ds(at, TILE), :] = jnp.where(same, 1.0, 0.0).astype(BF16)
+            hot[spot, pl.ds(at, TILE), :] = jnp.where(same, val[pl.ds(e, 1), :], 0.0).astype(BF16)
             return 0
 
         lax.fori_loop(0, tiles, mark, 0)
-        picked[...] = jnp.dot(hot[spot], tokens[...], preferred_element_type=F32).astype(BF16)
+        picked[...] = jnp.dot(plain[...], tokens[...], preferred_element_type=F32).astype(BF16)
 
         @pl.when(w == 0)
         def _():
@@ -436,9 +445,9 @@
             ).astype(BF16)
             return 0
 
-        lax.fori_loop(0, tiles // 2, functools.partial(tile, 1 - core_at), 0)
+        lax.fori_loop(0, tiles // 2, functools.partial(tile, 1 - core_at), 0, unroll=True)
         copy("swap", 0, w).start()
-        lax.fori_loop(0, tiles // 2, functools.partial(tile, core_at), 0)
+        lax.fori_loop(0, tiles // 2, functools.partial(tile, core_at), 0, unroll=True)
 
     def fold(w, step):
         at = pl.ds(pl.multiple_of(lax.rem(y + step, SIDE) * rows, rows), rows)
@@ -490,25 +499,16 @@
 
     def consume(w):
         spot = lax.rem(w, DEPTH)
-
-        @pl.when(w == 0)
-        def _():
-            for load in loads[experts:]:
-                load.wait()
-
         for step in (4, 1, 3, 2):
             copy("cross", step, w).wait_recv()
 
         def tile(j, _):
             e = table[w * tiles + j]
             at = pl.ds(pl.multiple_of(j * TILE, TILE), TILE)
-            result = lax.dot_general(
-                hidden[w, at, :], narrow[e], (((1,), (1,)), ((), ())), preferred_element_type=F32
-            )
-            turned[at, :] = result * scale[spot, at, :]
+            turned[at, :] = jnp.dot(hidden[w, at, :], flipped[e], preferred_element_type=F32)
             return 0
 
-        lax.fori_loop(0, tiles, tile, 0)
+        lax.fori_loop(0, tiles, tile, 0, unroll=True)
         flat = turned[...].T.astype(BF16)
         for c in range(pos.shape[1] // LANES):
             lane = pl.ds(c * LANES, LANES)
@@ -524,6 +524,16 @@
             @pl.when((w >= 0) & (w < waves))
             def _(late=late, w=w):
                 stages[late](w)
+
+        @pl.when(t == 0)
+        def _():
+            for load in loads[experts:]:
+                load.wait()
+
+        @pl.when(t < 4)
+        def _():
+            for e in (2 * t, 2 * t + 1):
+                flipped[e] = narrow[e].astype(F32).T.astype(BF16)
 
         return 0
 
@@ -560,9 +570,10 @@
         scratch_shapes=[
             pltpu.VMEM(gate_up.shape, BF16),
             pltpu.VMEM(down.shape, BF16),
+            pltpu.VMEM((experts, units, depth), BF16),
             pltpu.SemaphoreType.DMA((2 * experts,)),
             pltpu.VMEM((DEPTH, WAVE, total), BF16),
-            pltpu.VMEM((DEPTH, WAVE, 1), F32),
+            pltpu.VMEM((WAVE, total), BF16),
             pltpu.VMEM((WAVE, depth), BF16),
             pltpu.VMEM((waves, WAVE, width), BF16),
             pltpu.VMEM((waves, WAVE // 2, width), BF16),
@@ -586,26 +597,29 @@
 def local(tokens, gate_up_weight, down_weight, placement, copy_ids, gate_codes):
     steps, rows, depth = tokens.shape
     experts = gate_up_weight.shape[0]
-    top = copy_ids.shape[2]
     peers = lax.axis_size("ep")
-    own = lax.axis_index("ep").astype(I32).reshape(1)
-    raw = (copy_ids * 16 + gate_codes).reshape(steps * rows, top).T
-    codes, everyone = call_share(raw, placement, tokens.reshape(steps * rows, depth))
-    codes = codes.reshape(peers, top, steps * rows)
+    everyone, pos, val, table, most, totals = call_share(
+        copy_ids.transpose(0, 2, 1),
+        gate_codes.transpose(0, 2, 1),
+        placement,
+        tokens.reshape(steps * rows, depth),
+        experts,
+    )
     everyone = everyone.reshape(peers * steps * rows, depth)
+    most = most[0, 0]
+    table = table.reshape(-1)
+    tiles = CHOICES[-1] * WAVE // TILE
 
     def chunk(base, waves):
-        pos, val, table, _ = call_route(own, base.reshape(1), codes, experts)
-        return call_core(waves, table.reshape(-1), pos, val, everyone, gate_up_weight, down_weight)
-
-    pos, val, table, most = call_route(own, jnp.zeros((1,), I32), codes, experts)
-    most = most[0, 0]
+        part = lax.dynamic_slice(table, (base // TILE,), (tiles,))
+        return call_core(waves, part, pos - base, val, everyone, gate_up_weight, down_weight)
+
     branches = [functools.partial(call_core, waves) for waves in CHOICES]
     pick = jnp.int32(0)
     for waves in CHOICES[:-1]:
         pick += (most > waves * WAVE).astype(I32)
     mixed = lax.switch(
-        pick, branches, table.reshape(-1), pos, val, everyone, gate_up_weight, down_weight
+        pick, branches, table[:tiles], pos, val, everyone, gate_up_weight, down_weight
     )
     span = CHOICES[-1] * WAVE
     _, mixed = lax.while_loop(
@@ -617,8 +631,7 @@
         (jnp.int32(1), mixed),
     )
     mixed = call_settle(mixed.reshape(SIDE, SIDE, steps * rows, depth))
-    total = jnp.sum(gate_codes, axis=2).astype(F32)
-    return (mixed.reshape(steps, rows, depth) / total[:, :, None]).astype(BF16)
+    return (mixed.reshape(steps, rows, depth) / totals[:, :, None]).astype(BF16)
 
 
 def solution(mesh):

time: 115 us -> 116 us (level)
  Pallas kernels: 109 us -> 113 us
    pallas_call x1, Pallas kernels: 69.7 us -> 72.4 us  [call_core(): pl.pallas_call(functools.partial(core, waves), out_shape=jax.ShapeDtypeSt...]
    pallas_call x2 -> x1, Pallas kernels: 21.9 us -> 22.8 us  [call_share(): pl.pallas_call(share, out_shape=(jax.ShapeDtypeStruct((peers,) + tokens.s...]
where the time goes in v5:
time: 116 us
  Pallas kernels  113 us (97%)
  other arithmetic  1.67 us (1%)
    pallas_call x1, Pallas kernels, call_core(): pl.pallas_call(functools.partial(core, waves), out_shape=jax.ShapeDtypeSt...  72.4 us
    pallas_call x1, Pallas kernels, call_share(): pl.pallas_call(share, out_shape=(jax.ShapeDtypeStruct((peers,) + tokens.s...  22.8 us
    pallas_call x1, Pallas kernels, call_settle(): pl.pallas_call(settle, out_shape=jax.ShapeDtypeStruct((rows, depth), F32)...  17.8 us

profile of v5, /device:TPU:8, one launch (start us, length us, event | category | flops | bytes accessed | tf_op | source)
XLA Modules:
  0.0 116.1 jit_solution(8963829965647319724)
XLA Ops:
  0.0 22.8 %share.1 = (bf16[16,192,256]{2,1,0:T(8,128)(2,1)S(1)}, s32[8,3072]{1,0:T(8,128)S(1)}, f32[8,3072]{1,0:T(8,128)S(1)}, s32[1,512]{1,0:T(1,128)S(1)}, s32[1,128]{1,0:T(1,128)S(1)}, /*index=5*/f32[4,48]{1,0:T(4,128)}) custom-call(s32[4,8,48]{2,1,0:T(8,128)} %bitcast.19, s32[4,8,48]{2,1,0:T(8,128)} %bitcast.20, s32[160]{0:T(256)} %placement.1, ...), custom_call_target="tpu_custom_call" | custom-call | tf_op jit(solution)/shard_map/share/pallas_call | solution.py:221
  22.8 0.0 copy-start.1
  22.9 0.4 copy-done.1
  23.3 72.6 %conditional.1 = (bf16[3072,256]{1,0:T(8,128)(2,1)}) conditional(s32[]{:T(128)} %clamp.3, (s32[80]{0:T(128)S(1)}, s32[8,3072]{1,0:T(8,128)S(1)}, f32[8,3072]{1,0:T(8,128)S(1)}, bf16[3072,256]{1,0:T(8,128)(2,1)S(1)}, bf16[8,256,1536]{2,1,0:T(8,128)(2,1)}, /*index=5*/bf16[8,256,768]{2,1,0:T(8,128)(2,1)}) %tuple.46, ...), branch_computations={%region_0.0_spmd, %region_1.0_spmd, %region_2.0_spmd, %region_3.0_... | conditional | bytes 8 | solution.py:621
  23.3 72.4 %core9.1 = bf16[3072,256]{1,0:T(8,128)(2,1)} custom-call(s32[80]{0:T(128)S(1)} %get-tuple-element.171.table, s32[8,3072]{1,0:T(8,128)S(1)} %get-tuple-element.172.pos, f32[8,3072]{1,0:T(8,128)S(1)} %get-tuple-element.173.val, bf16[3072,256]{1,0:T(8,128)(2,1)S(1)} %get-tuple-element.174.tokens, bf16[8,256,1536]{2,1,0:T(8,128)(2,1)} %get-tuple-element.175.gate_up, ...), custom_call_target="tpu_custom_call" | custom-call | tf_op jit(solution)/shard_map/cond/branch_2_fun/core9/pallas_call | solution.py:565
  96.0 0.6 while.12
  96.6 0.0 copy-start
  96.6 17.8 %settle.1 = f32[192,256]{1,0:T(8,128)} custom-call(bf16[4,4,192,256]{3,2,1,0:T(8,128)(2,1)} %bitcast.16), custom_call_target="tpu_custom_call" | custom-call | tf_op jit(solution)/shard_map/settle/pallas_call | solution.py:301
  114.4 0.0 copy-done
  114.4 1.7 %divide_convert_fusion = bf16[4,48,256]{2,1,0:T(8,128)(2,1)} fusion(f32[4,48,256]{2,1,0:T(8,128)} %bitcast.17, f32[4,48]{1,0:T(4,128)S(1)} %copy-done), kind=kLoop, calls=%fused_computation.2 | loop fusion | flops 98304 | bytes 295680 | tf_op jit(solution)/shard_map/convert_element_type | solution.py:634
  (1 shorter events, 0.0 us)
Async XLA Ops:
  22.8 0.6 copy-start.1
  96.6 17.8 %copy-start = (f32[4,48]{1,0:T(4,128)S(1)}, f32[4,48]{1,0:T(4,128)}, u32[]{:S(2)}) copy-start(f32[4,48]{1,0:T(4,128)} %get-tuple-element.207) | copy-start | bytes 2308

commit v6 on v5

--- a/solution.py
+++ b/solution.py
@@ -96,8 +96,15 @@
     named = jnp.zeros((peers, experts), F32)
     owner_of = lax.broadcasted_iota(I32, (peers, code.shape[1]), 0)
     local_of = lax.broadcasted_iota(I32, (experts, code.shape[1]), 0)
+    every = code >> 4
+    again = jnp.zeros(every.shape, I32)
+    choice = lax.broadcasted_iota(I32, every.shape, 0)
+    for step in range(1, every.shape[0]):
+        same = (pltpu.roll(every, step, 0) == every) & (choice >= step)
+        again = jnp.where(same, 1, again)
+    every = jnp.where(again > 0, peers * experts, every)
     for k in range(code.shape[0]):
-        expert = code[k : k + 1, :] >> 4
+        expert = every[k : k + 1, :]
         owner = lax.div(expert, experts)
         named = named + lax.dot_general(
             (owner == owner_of).astype(F32).astype(BF16),
@@ -241,9 +248,13 @@
     )(ids, gates, placement, tokens)
 
 
-def settle(parts, out, big, fills, sums, small, sends, recvs):
+def ep_peers():
     me, z, x, at = torus()
-    greet([{"ep": at(0, step)} for step in (1, 2, 3)] + [{"ep": at(step, 0)} for step in (1, 2, 3)])
+    return [{"ep": at(0, step)} for step in (1, 2, 3)] + [{"ep": at(step, 0)} for step in (1, 2, 3)]
+
+
+def settle(out, acc, parts, big, fills, sums, small, sends, recvs):
+    me, z, x, at = torus()
     rows, depth = parts.shape[2:]
     half, lot = depth // 2, rows // 2
     post = Post(sends, recvs)
@@ -259,7 +270,17 @@
         along_x = (side == 0) == (stage == 1)
         return {"ep": at(0, step) if along_x else at(step, 0)}
 
+    def flip(far, pair):
+        lane = pl.multiple_of((far * 2 + pair) * 2 * rows, 2 * rows)
+        turned = acc[:, pl.ds(lane, 2 * rows)].T.astype(BF16)
+        for near in (0, 1):
+            parts[far, pair * 2 + near] = turned[near * rows : (near + 1) * rows]
+
     for side in (0, 1):
+        if acc is not None:
+            pair = lax.div(lax.rem(x + (2 if side == 0 else 0), SIDE), 2)
+            for far in range(SIDE):
+                flip(far, pair)
         post.send((side, 0), wide(side, 2, LOW), big.at[side, 0], target(side, 1, 1))
         post.send((side, 1), wide(side, 2, HIGH), big.at[side, 1], target(side, 1, 3))
     for side in (0, 1):
@@ -294,23 +315,33 @@
     post.drain()
 
 
+def settle_scratch(rows, depth):
+    lot, half = rows // 2, depth // 2
+    return [
+        pltpu.VMEM((SIDE, SIDE, rows, depth), BF16),
+        pltpu.VMEM((2, 6, SIDE, lot, half), BF16),
+        pltpu.VMEM((2, 2, SIDE, lot, half), BF16),
+        pltpu.VMEM((2, SIDE, rows, half), BF16),
+        pltpu.VMEM((2, 3, rows, half), BF16),
+        pltpu.SemaphoreType.DMA((18,)),
+        pltpu.SemaphoreType.DMA((18,)),
+    ]
+
+
+def settle_alone(parts, out, *scratch):
+    greet(ep_peers())
+    settle(out, None, parts, *scratch)
+
+
 def call_settle(parts):
     rows, depth = parts.shape[2:]
-    lot, half = rows // 2, depth // 2
     vmem = pl.BlockSpec(memory_space=pltpu.VMEM)
     return pl.pallas_call(
-        settle,
+        settle_alone,
         out_shape=jax.ShapeDtypeStruct((rows, depth), F32),
         in_specs=[vmem],
         out_specs=vmem,
-        scratch_shapes=[
-            pltpu.VMEM((2, 6, SIDE, lot, half), BF16),
-            pltpu.VMEM((2, 2, SIDE, lot, half), BF16),
-            pltpu.VMEM((2, SIDE, rows, half), BF16),
-            pltpu.VMEM((2, 3, rows, half), BF16),
-            pltpu.SemaphoreType.DMA((18,)),
-            pltpu.SemaphoreType.DMA((18,)),
-        ],
+        scratch_shapes=settle_scratch(rows, depth)[1:],
         compiler_params=pltpu.CompilerParams(collective_id=2, has_side_effects=True),
         name="settle",
     )(parts)
@@ -353,6 +384,7 @@
     acc,
     sends,
     recvs,
+    *rest,
 ):
     me = lax.axis_index("fsdp")
     y, core_at = lax.div(me, 2), lax.rem(me, 2)
@@ -369,7 +401,7 @@
         loads.append(pltpu.make_async_copy(down.at[e], narrow.at[e], wsems.at[experts + e]))
     for load in loads:
         load.start()
-    greet([partner, sides[1], sides[3]])
+    greet([partner, sides[1], sides[3]] + (ep_peers() if rest else []))
     columns = (pl.ds(0, units), pl.ds(units, units))
 
     def half(which):
@@ -539,22 +571,26 @@
 
     lax.fori_loop(0, waves + len(stages) - 1, turn, 0)
 
+    def drain(w, _):
+        for name, step in KINDS:
+            copy(name, step, w).wait_send()
+        return 0
+
+    if rest:
+        settle(out, acc, *rest)
+        lax.fori_loop(0, waves, drain, 0)
+        return
+
     def flip(c, _):
         lane = pl.multiple_of(c * 256, 256)
         out[pl.ds(lane, 256), :] = acc[:, pl.ds(lane, 256)].T.astype(out.dtype)
         return 0
 
     lax.fori_loop(0, out.shape[0] // 256, flip, 0)
-
-    def drain(w, _):
-        for name, step in KINDS:
-            copy(name, step, w).wait_send()
-        return 0
-
     lax.fori_loop(0, waves, drain, 0)
 
 
-def call_core(waves, table, pos, val, tokens, gate_up, down):
+def call_core(waves, fused, table, pos, val, tokens, gate_up, down):
     experts, depth, width = gate_up.shape
     rows, units = WAVE // 8, width // 2
     total = tokens.shape[0]
@@ -564,7 +600,9 @@
     piece = pltpu.VMEM((waves, 2, rows, units), BF16)
     return pl.pallas_call(
         functools.partial(core, waves),
-        out_shape=jax.ShapeDtypeStruct((total, depth), BF16),
+        out_shape=jax.ShapeDtypeStruct(
+            (total // (SIDE * SIDE), depth) if fused else (total, depth), F32 if fused else BF16
+        ),
         in_specs=[smem, vmem, vmem, vmem, hbm, hbm],
         out_specs=vmem,
         scratch_shapes=[
@@ -586,11 +624,12 @@
             pltpu.VMEM((depth, total), F32),
             pltpu.SemaphoreType.DMA((waves, len(KINDS))),
             pltpu.SemaphoreType.DMA((waves, len(KINDS))),
-        ],
+        ]
+        + (settle_scratch(total // (SIDE * SIDE), depth) if fused else []),
         compiler_params=pltpu.CompilerParams(
-            collective_id=waves, has_side_effects=True, vmem_limit_bytes=62 << 20
+            collective_id=waves + (0 if fused else 16), has_side_effects=True, vmem_limit_bytes=62 << 20
         ),
-        name="core%d" % waves,
+        name="core%d" % waves + ("s" if fused else ""),
     )(table, pos, val, tokens, gate_up, down)
 
 
@@ -610,27 +649,28 @@
     table = table.reshape(-1)
     tiles = CHOICES[-1] * WAVE // TILE
 
-    def chunk(base, waves):
-        part = lax.dynamic_slice(table, (base // TILE,), (tiles,))
-        return call_core(waves, part, pos - base, val, everyone, gate_up_weight, down_weight)
-
-    branches = [functools.partial(call_core, waves) for waves in CHOICES]
+    span = CHOICES[-1] * WAVE
+
+    def usual(waves, *operands):
+        return call_core(waves, True, operands[0][:tiles], *operands[1:])
+
+    def beyond(table, pos, *operands):
+        def chunk(at):
+            part = lax.dynamic_slice(table, (at * tiles,), (tiles,))
+            return call_core(CHOICES[-1], False, part, pos - at * span, *operands)
+
+        _, sums = lax.while_loop(
+            lambda c: c[0] * span < most,
+            lambda c: (c[0] + 1, (c[1].astype(F32) + chunk(c[0]).astype(F32)).astype(BF16)),
+            (jnp.int32(0), jnp.zeros((peers * steps * rows, depth), BF16)),
+        )
+        return call_settle(sums.reshape(SIDE, SIDE, steps * rows, depth))
+
+    branches = [functools.partial(usual, waves) for waves in CHOICES] + [beyond]
     pick = jnp.int32(0)
-    for waves in CHOICES[:-1]:
+    for waves in CHOICES:
         pick += (most > waves * WAVE).astype(I32)
-    mixed = lax.switch(
-        pick, branches, table[:tiles], pos, val, everyone, gate_up_weight, down_weight
-    )
-    span = CHOICES[-1] * WAVE
-    _, mixed = lax.while_loop(
-        lambda c: c[0] * span < most,
-        lambda c: (
-            c[0] + 1,
-            (c[1].astype(F32) + chunk(c[0] * span, CHOICES[-1]).astype(F32)).astype(BF16),
-        ),
-        (jnp.int32(1), mixed),
-    )
-    mixed = call_settle(mixed.reshape(SIDE, SIDE, steps * rows, depth))
+    mixed = lax.switch(pick, branches, table, pos, val, everyone, gate_up_weight, down_weight)
     return (mixed.reshape(steps, rows, depth) / totals[:, :, None]).astype(BF16)
 
 

time: 116 us -> 109 us (0.940)
  Pallas kernels: 113 us -> 106 us
    pallas_call x1 -> x0, Pallas kernels: 17.8 us -> none  [call_settle(): pl.pallas_call(settle, out_shape=jax.ShapeDtypeStruct((rows, depth), F32)...]
    pallas_call x1, Pallas kernels: 72.4 us -> 83.5 us  [call_core(): pl.pallas_call(functools.partial(core, waves), out_shape=jax.ShapeDtypeSt...]
where the time goes in v6:
time: 109 us; the launch traced here: 108 us
  Pallas kernels  106 us (97%)
    pallas_call x1, Pallas kernels, call_core(): pl.pallas_call(functools.partial(core, waves), out_shape=jax.ShapeDtypeSt...  83.5 us
    pallas_call x1, Pallas kernels, call_share(): pl.pallas_call(share, out_shape=(jax.ShapeDtypeStruct((peers,) + tokens.s...  22.8 us

profile of v6, /device:TPU:8, one launch (start us, length us, event | category | flops | bytes accessed | tf_op | source)
XLA Modules:
  0.0 108.1 jit_solution(5269007498534437132)
XLA Ops:
  0.0 22.8 %share.1 = (bf16[16,192,256]{2,1,0:T(8,128)(2,1)S(1)}, s32[8,3072]{1,0:T(8,128)S(1)}, f32[8,3072]{1,0:T(8,128)S(1)}, s32[1,512]{1,0:T(1,128)S(1)}, s32[1,128]{1,0:T(1,128)S(1)}, /*index=5*/f32[4,48]{1,0:T(4,128)}) custom-call(s32[4,8,48]{2,1,0:T(8,128)} %bitcast.25, s32[4,8,48]{2,1,0:T(8,128)} %bitcast.26, s32[160]{0:T(256)} %placement.1, ...), custom_call_target="tpu_custom_call" | custom-call | tf_op jit(solution)/shard_map/share/pallas_call | solution.py:228
  22.9 0.0 copy-start
  22.9 84.4 %conditional.1 = (f32[4,48,256]{2,1,0:T(8,128)S(1)}) conditional(s32[]{:T(128)} %clamp.3, (s32[512]{0:T(512)S(1)}, s32[8,3072]{1,0:T(8,128)S(1)}, f32[8,3072]{1,0:T(8,128)S(1)}, bf16[3072,256]{1,0:T(8,128)(2,1)S(1)}, bf16[8,256,1536]{2,1,0:T(8,128)(2,1)}, /*index=5*/bf16[8,256,768]{2,1,0:T(8,128)(2,1)}) %tuple.52, ...), branch_computations={%region_0.0_spmd, %region_1.0_spmd, %region_2.0_spmd, %region_3.0_... | conditional | flops 3170312 | bytes 6489097 | solution.py:673
  23.2 0.5 slice.12.table
  23.7 83.5 %core9s.1 = f32[192,256]{1,0:T(8,128)S(1)} custom-call(s32[80]{0:T(128)} %slice.12.table, s32[8,3072]{1,0:T(8,128)S(1)} %get-tuple-element.123.pos, f32[8,3072]{1,0:T(8,128)S(1)} %get-tuple-element.124.val, bf16[3072,256]{1,0:T(8,128)(2,1)S(1)} %get-tuple-element.125.tokens, bf16[8,256,1536]{2,1,0:T(8,128)(2,1)} %get-tuple-element.126.gate_up, ...), custom_call_target="tpu_custom_call" | custom-call | tf_op jit(solution)/shard_map/cond/branch_2_fun/core9s/pallas_call | solution.py:601
  107.4 0.0 copy-done
  107.4 0.7 divide_convert_fusion
Async XLA Ops:
  22.9 84.4 %copy-start = (f32[4,48]{1,0:T(4,128)S(1)}, f32[4,48]{1,0:T(4,128)}, u32[]{:S(2)}) copy-start(f32[4,48]{1,0:T(4,128)} %get-tuple-element.164) | copy-start | bytes 2308
